TPU v7x, 512 devices: a whole 4x8x8 slice. The times are simulated.
512 devices in a mesh: dp: 4 (over x), section: 8 (over y), tensor: 16 (over z, core).
Axes of the slice: x: 4, y: 8, z: 8, core: 2. Of those that a mesh axis runs over, the one named last changes fastest.
Arguments:
- arrivals: bfloat16 [8, 4, 128, 4096], P('section', 'dp', None, 'tensor'), may hold values from -30 to 30
- fresh: bfloat16 [2, 4, 128, 4096], P(None, 'dp', None, 'tensor'), may hold values from -30 to 30
- stash: bfloat16 [2, 8, 4, 128, 4096], P(None, 'section', 'dp', None, 'tensor'), may hold values from -30 to 30
- returning: bfloat16 [8, 4, 128, 4096], P('section', 'dp', None, 'tensor'), may hold values from -6 to 6
- loss_grad: bfloat16 [2, 4, 128, 4096], P(None, 'dp', None, 'tensor'), may hold values from -6 to 6
- gain: float32 [8, 4096], P('section', 'tensor'), may hold values from 0.1 to 1.9
- query_weight: bfloat16 [8, 4096, 4096], P('section', 'dp', 'tensor'), may hold values from -0.09375 to 0.09375
- key_weight: bfloat16 [8, 4096, 1024], P('section', 'dp', 'tensor'), may hold values from -0.09375 to 0.09375
- value_weight: bfloat16 [8, 4096, 1024], P('section', 'dp', 'tensor'), may hold values from -0.09375 to 0.09375
- w_out: bfloat16 [8, 4096, 4096], P('section', 'dp', 'tensor'), may hold values from -0.09375 to 0.09375
- plan: int32 [2, 4], replicated, may hold values from 0 to 3, each once within a row
- fresh_docs: int32 [2, 4, 128], replicated, may hold values from 0 to 5, never falling along the last dimension, each value on 1 to 64 neighbouring positions
- arrival_docs: int32 [8, 4, 128], P(None, 'dp'), may hold values from 0 to 5, never falling along the last dimension, each value on 1 to 64 neighbouring positions
- stash_docs: int32 [2, 8, 4, 128], P(None, 'section', 'dp'), may hold values from 0 to 5, never falling along the last dimension, each value on 1 to 64 neighbouring positions
Outputs:
- sent_forward: bfloat16 [8, 4, 128, 4096], P('section', 'dp', None, 'tensor')
- sent_backward: bfloat16 [8, 4, 128, 4096], P('section', 'dp', None, 'tensor')
- gain_grad: float32 [8, 4096], P('section', 'tensor')
Inputs may be any that keep to these rules, and one draw needn't show every extreme that they name: Each row of plan names every packed row of its micro-batch once. `fresh_docs`: along a packed row document numbers never fall; every document holds 1 to 64 tokens and one holds exactly 64. `arrival_docs`: along a packed row document numbers never fall; every document holds 1 to 64 tokens and one holds exactly 64. `stash_docs`: along a packed row document numbers never fall; every document holds 1 to 64 tokens and one holds exactly 64.
All inputs are finite; a program needn't handle non-finite values.
Results may differ from a plain program's by a relative error of at most 0.035.
Values may be sent and summed in bfloat16 or wider, within the bound.
A program may use at most 64 MiB of HBM per device.

v0:
```python
import math

import jax
import jax.numpy as jnp
from jax import lax
from jax.sharding import PartitionSpec as P

MODEL_WIDTH = 4096
QUERY_HEADS = 32
KEY_VALUE_HEADS = 8
HEAD_SIZE = 128
TICKS = 2


norm_eps = 1e-05


def partner_2(block, axis, bit):
    count = lax.axis_size(axis)
    route = []
    for low in range(count):
        high = low | 1 << bit
        if high != low and high < count:
            route += [(low, high), (high, low)]
    return lax.ppermute(block, axis, route)


def from_behind(value, axis, steps):
    count = lax.axis_size(axis)
    leading, last = (max(0, -steps), min(count, count - steps))
    return lax.ppermute(value, axis, [(source, source + steps) for source in range(leading, last)])


def document_mask(documents):
    length = documents.shape[-1]
    same = documents[:, :, None] == documents[:, None, :]
    causal = jnp.arange(length)[:, None] >= jnp.arange(length)[None, :]
    return jnp.logical_and(same, causal[None])[:, None, None]


def attention_probs(query_rows, key_rows, value_rows, documents, kv_heads):
    rows, length = documents.shape
    per_key = query_rows.shape[1] // (kv_heads * HEAD_SIZE)
    query_heads = query_rows.reshape(rows, length, kv_heads, per_key, HEAD_SIZE)
    heads_of_key = key_rows.reshape(rows, length, kv_heads, HEAD_SIZE)
    heads_of_value = value_rows.reshape(rows, length, kv_heads, HEAD_SIZE)
    scores = jnp.einsum(
        "rikgd,rjkd->rkgij", query_heads, heads_of_key, preferred_element_type=jnp.float32
    ) * HEAD_SIZE ** (-0.5)
    raised = jnp.where(document_mask(documents), jnp.exp(scores), 0.0)
    probs = raised / jnp.sum(raised, axis=-1, keepdims=True)
    return (query_heads, heads_of_key, heads_of_value, probs, probs.astype(jnp.bfloat16))


def local(
    arrivals,
    fresh,
    stash,
    returning,
    loss_grad,
    gain,
    query_weight,
    key_weight,
    value_weight,
    w_out,
    plan,
    fresh_docs,
    arrival_docs,
    stash_docs,
):
    tensor_count = lax.axis_size("tensor")
    section_count = lax.axis_size("section")
    replicas = lax.axis_size("dp")
    tensor_pos = lax.axis_index("tensor")
    section_pos = lax.axis_index("section")
    replica_pos = lax.axis_index("dp")
    rows, length, width = (arrivals.shape[1], arrivals.shape[2], arrivals.shape[3])
    tokens = rows * length
    heads_here = QUERY_HEADS // tensor_count
    group_width = QUERY_HEADS // KEY_VALUE_HEADS
    share_count = max(1, group_width // heads_here)
    bit_count = share_count.bit_length() - 1
    query_cols = heads_here * HEAD_SIZE
    query_w, key_w, value_w, out_w = (
        lax.all_gather(query_weight[0], "dp", axis=0, tiled=True),
        lax.all_gather(key_weight[0], "dp", axis=0, tiled=True),
        lax.all_gather(value_weight[0], "dp", axis=0, tiled=True),
        lax.all_gather(w_out[0], "dp", axis=0, tiled=True),
    )
    grad_weights = jnp.concatenate([query_w, key_w, value_w], axis=1)
    paired = jnp.stack([key_w, value_w])
    bit_pos = 0
    partner = partner_2(paired, "tensor", bit_pos)
    low_side = tensor_pos >> bit_pos & 1 == 0
    paired = jnp.where(
        low_side, jnp.concatenate([paired, partner], -1), jnp.concatenate([partner, paired], -1)
    )
    forward_weights = jnp.concatenate([query_w, paired[0], paired[1]], axis=1)
    key_columns = (forward_weights.shape[1] - query_cols) // 2
    gathered = lax.all_gather(fresh, "dp", axis=1, tiled=True)
    sources = lax.dynamic_slice_in_dim(plan, replica_pos * rows, rows, 1)
    fresh_rows = jnp.stack(
        [jnp.take(gathered[tick], sources[tick], axis=0) for tick in range(TICKS)]
    )
    fresh_documents = jnp.stack(
        [jnp.take(fresh_docs[tick], sources[tick], axis=0) for tick in range(TICKS)]
    )
    gain_row = gain[0]
    outgoing = arrivals[0]
    going_back = returning[0]
    gain_total = jnp.zeros((width,), jnp.float32)
    for tick in range(TICKS):
        incoming = from_behind(outgoing, "section", 1)
        forward_in = jnp.where(section_pos == 0, fresh_rows[tick], incoming).reshape(tokens, width)
        from_arrivals = lax.dynamic_index_in_dim(
            arrival_docs, jnp.clip(section_pos - tick - 1, 0, section_count - 1), 0, keepdims=False
        )
        from_fresh = lax.dynamic_index_in_dim(
            fresh_documents, jnp.clip(tick - section_pos, 0, TICKS - 1), 0, keepdims=False
        )
        forward_docs = jnp.where(section_pos > tick, from_arrivals, from_fresh)
        arriving = from_behind(going_back, "section", -1)
        grad_in = jnp.where(section_pos == section_count - 1, loss_grad[tick], arriving).reshape(
            tokens, width
        )
        backward_in = stash[tick, 0].reshape(tokens, width)
        backward_docs = stash_docs[tick, 0]
        forward_f = forward_in.astype(jnp.float32)
        backward_f = backward_in.astype(jnp.float32)
        forward_sq, backward_sq = lax.psum(
            (jnp.sum(forward_f * forward_f, -1), jnp.sum(backward_f * backward_f, -1)), "tensor"
        )
        forward_inv = lax.rsqrt(forward_sq / MODEL_WIDTH + norm_eps)
        backward_inv = lax.rsqrt(backward_sq / MODEL_WIDTH + norm_eps)
        forward_normed = (forward_f * forward_inv[:, None] * gain_row).astype(jnp.bfloat16)
        backward_normed = (backward_f * backward_inv[:, None] * gain_row).astype(jnp.bfloat16)
        forward_proj = jnp.dot(
            lax.all_gather(forward_normed, "tensor", axis=1, tiled=True),
            forward_weights,
            preferred_element_type=jnp.float32,
        )
        backward_proj = jnp.dot(
            lax.all_gather(backward_normed, "tensor", axis=1, tiled=True),
            forward_weights,
            preferred_element_type=jnp.float32,
        )
        forward_proj = forward_proj.astype(jnp.bfloat16)
        backward_proj = backward_proj.astype(jnp.bfloat16)
        forward_query = forward_proj[:, :query_cols]
        forward_key = forward_proj[:, query_cols : query_cols + key_columns]
        forward_value = forward_proj[:, query_cols + key_columns :]
        backward_query = backward_proj[:, :query_cols]
        backward_key = backward_proj[:, query_cols : query_cols + key_columns]
        backward_value = backward_proj[:, query_cols + key_columns :]
        kv_heads = forward_key.shape[1] // HEAD_SIZE
        fwd_parts = attention_probs(
            forward_query, forward_key, forward_value, forward_docs, kv_heads
        )
        mixed = jnp.einsum(
            "rkgij,rjkd->rikgd", fwd_parts[4], fwd_parts[2], preferred_element_type=jnp.float32
        )
        mixed = mixed.astype(jnp.bfloat16).reshape(tokens, query_cols)
        attended = jnp.dot(
            lax.all_gather(mixed, "tensor", axis=1, tiled=True),
            out_w,
            preferred_element_type=jnp.float32,
        )
        outgoing = (forward_f + attended).astype(jnp.bfloat16).reshape(rows, length, width)
        query_heads, heads_of_key, heads_of_value, probs, probs_half = attention_probs(
            backward_query, backward_key, backward_value, backward_docs, kv_heads
        )
        head_gradient = lax.psum_scatter(
            lax.dot_general(
                out_w, grad_in, (((1,), (1,)), ((), ())), preferred_element_type=jnp.float32
            ).astype(jnp.bfloat16),
            "tensor",
            scatter_dimension=0,
            tiled=True,
        ).astype(jnp.float32)
        head_gradient = head_gradient.T.astype(jnp.bfloat16).reshape(query_heads.shape)
        prob_grad = jnp.einsum(
            "rikgd,rjkd->rkgij", head_gradient, heads_of_value, preferred_element_type=jnp.float32
        )
        score_grad = (
            probs
            * (prob_grad - jnp.sum(probs * prob_grad, axis=-1, keepdims=True))
            * HEAD_SIZE ** (-0.5)
        ).astype(jnp.bfloat16)
        query_grad = jnp.einsum(
            "rkgij,rjkd->rikgd", score_grad, heads_of_key, preferred_element_type=jnp.float32
        )
        query_grad = query_grad.astype(jnp.bfloat16).reshape(tokens, query_cols)
        key_grad = jnp.einsum(
            "rkgij,rikgd->rjkd", score_grad, query_heads, preferred_element_type=jnp.float32
        ).reshape(tokens, -1)
        value_grad = jnp.einsum(
            "rkgij,rikgd->rjkd", probs_half, head_gradient, preferred_element_type=jnp.float32
        ).reshape(tokens, -1)
        kv_grad = jnp.stack([key_grad, value_grad])
        for bit_pos in reversed(range(bit_count)):
            half = kv_grad.shape[-1] // 2
            low_side = tensor_pos >> bit_pos & 1 == 0
            keep = jnp.where(low_side, kv_grad[..., :half], kv_grad[..., half:])
            outward = jnp.where(low_side, kv_grad[..., half:], kv_grad[..., :half])
            kv_grad = keep + partner_2(outward.astype(jnp.bfloat16), "tensor", bit_pos).astype(
                outward.dtype
            )
        kv_grad = kv_grad.astype(jnp.bfloat16)
        grad_rows = jnp.concatenate([query_grad, kv_grad[0], kv_grad[1]], axis=1)
        normed_grad = (
            lax.psum_scatter(
                lax.dot_general(
                    grad_weights,
                    grad_rows,
                    (((1,), (1,)), ((), ())),
                    preferred_element_type=jnp.float32,
                ).astype(jnp.bfloat16),
                "tensor",
                scatter_dimension=0,
                tiled=True,
            )
            .astype(jnp.float32)
            .T
        )
        scaled = normed_grad * gain_row
        row_dot = lax.psum(jnp.sum(scaled * backward_f, -1), "tensor")
        result = (
            grad_in.astype(jnp.float32)
            + backward_inv[:, None] * scaled
            - backward_f * (backward_inv**3 * row_dot / MODEL_WIDTH)[:, None]
        )
        going_back = result.astype(jnp.bfloat16).reshape(rows, length, width)
        gain_total = gain_total + jnp.sum(normed_grad * backward_f * backward_inv[:, None], axis=0)
    gain_grad = lax.psum(gain_total, "dp") / math.sqrt(TICKS * rows * replicas * length)
    return (outgoing[None], going_back[None], gain_grad[None])


def solution(mesh):
    return jax.shard_map(
        local,
        mesh=mesh,
        in_specs=(
            P("section", "dp", None, "tensor"),
            P(None, "dp", None, "tensor"),
            P(None, "section", "dp", None, "tensor"),
            P("section", "dp", None, "tensor"),
            P(None, "dp", None, "tensor"),
            P("section", "tensor"),
            P("section", "dp", "tensor"),
            P("section", "dp", "tensor"),
            P("section", "dp", "tensor"),
            P("section", "dp", "tensor"),
            P(),
            P(),
            P(None, "dp", None),
            P(None, "section", "dp", None),
        ),
        out_specs=(
            P("section", "dp", None, "tensor"),
            P("section", "dp", None, "tensor"),
            P("section", "tensor"),
        ),
        check_vma=False,
    )
```

profile of v0, /device:TPU:1, one launch (start us, length us, event | category | flops | bytes accessed | tf_op | source)
XLA Modules:
  0.0 691.6 jit_solution(4623848368718102697)
XLA Ops:
  8.9 30.6 %psum.51 = f32[128]{0:T(128)S(1)} all-reduce(f32[128]{0:T(128)S(1)} %fusion.44), channel_id=1, replica_groups=mesh['dp'=4,'section'=8,'tensor'=16] {'tensor'}, use_global_device_ids=true, to_apply=%region_7.10 | all-reduce | flops 128 | bytes 1024 | tf_op jit(solution)/shard_map/psum | solution.py:130
  41.9 12.9 %all-gather.1 = bf16[1,4096,64]{1,2,0:T(8,128)(2,1)S(1)} all-gather(bf16[1,1024,64]{1,2,0:T(8,128)(2,1)} %param.25), channel_id=3, replica_groups=mesh['dp'=4,'section'=8,'tensor'=16] {'dp'}, dimensions={1}, use_global_device_ids=true | all-gather | bytes 655360 | tf_op jit(solution)/shard_map/all_gather | solution.py:86
  54.9 10.8 %all-gather.2 = bf16[1,4096,64]{1,2,0:T(8,128)(2,1)S(1)} all-gather(bf16[1,1024,64]{1,2,0:T(8,128)(2,1)} %param.26), channel_id=4, replica_groups=mesh['dp'=4,'section'=8,'tensor'=16] {'dp'}, dimensions={1}, use_global_device_ids=true | all-gather | bytes 655360 | tf_op jit(solution)/shard_map/all_gather | solution.py:87
  65.7 9.5 %collective-permute-start.1 = (bf16[2,4096,64]{1,2,0:T(8,128)(2,1)S(1)}, bf16[2,4096,64]{1,2,0:T(8,128)(2,1)S(1)}, u32[]{:S(2)}, u32[]{:S(2)}) collective-permute-start(bf16[2,4096,64]{1,2,0:T(8,128)(2,1)S(1)} %constant_dynamic-update-slice_fusion), channel_id=1, source_target_pairs={{0,1},{1,0},{2,3},{3,2},{4,5},{5,4},{6,7},{7,6},{8,9},{9,8},{10,11... | collective-permute-start | bytes 3145736 | tf_op jit(solution)/shard_map/ppermute | solution.py:25
  80.9 3.4 fusion
  86.4 13.7 %all-gather.21.cloned.1.call-done = bf16[128,4096]{1,0:T(8,128)(2,1)} async-done(((bf16[128,256]{1,0:T(8,128)(2,1)}), bf16[128,4096]{1,0:T(8,128)(2,1)}) %all-gather.21.cloned.1.call-update) | async-done | bytes 1048592 | tf_op jit(solution)/shard_map/all_gather | solution.py:143
  100.1 36.6 %all-gather.25.cloned.1.call-done = bf16[1,4096,256]{2,1,0:T(8,128)(2,1)} async-done(((bf16[1,1024,256]{2,1,0:T(8,128)(2,1)}), bf16[1,4096,256]{2,1,0:T(8,128)(2,1)}) %all-gather.25.cloned.1.call-update) | async-done | bytes 2097168 | tf_op jit(solution)/shard_map/all_gather | solution.py:85
  136.7 2.7 convolution_convert_fusion.5
  141.3 56.0 %reduce-scatter.5.cloned.1.call-done = bf16[256,128]{0,1:T(8,128)(2,1)} async-done(((bf16[4096,128]{0,1:T(8,128)(2,1)}), bf16[256,128]{0,1:T(8,128)(2,1)}) %reduce-scatter.5.cloned.1.call-update) | async-done | bytes 65552 | tf_op jit(solution)/shard_map/reduce_scatter | solution.py:172
  199.6 5.4 collective-permute-start.4
  206.1 4.0 convolution_convert_fusion.2
  210.2 3.2 collective-permute-start
  213.5 11.4 %all_gather.33 = bf16[2,4,128,256]{3,2,1,0:T(8,128)(2,1)S(1)} all-gather(bf16[2,1,128,256]{3,2,1,0:T(8,128)(2,1)} %param.19), channel_id=1, replica_groups=mesh['dp'=4,'section'=8,'tensor'=16] {'dp'}, dimensions={1}, use_global_device_ids=true | all-gather | bytes 655360 | tf_op jit(solution)/shard_map/all_gather | solution.py:100
  228.9 36.8 %reduce-scatter.7.cloned.1.call-done = bf16[256,128]{0,1:T(8,128)(2,1)} async-done(((bf16[4096,128]{0,1:T(8,128)(2,1)}), bf16[256,128]{0,1:T(8,128)(2,1)}) %reduce-scatter.7.cloned.1.call-update) | async-done | bytes 65552 | tf_op jit(solution)/shard_map/reduce_scatter | solution.py:211
  267.3 26.9 %all-reduce.1 = (f32[128]{0:T(128)}, f32[128]{0:T(128)}, f32[128]{0:T(128)}) all-reduce(f32[128]{0:T(128)S(1)} %get-tuple-element.39, f32[128]{0:T(128)} %get-tuple-element.30, f32[128]{0:T(128)} %get-tuple-element.31), channel_id=1, replica_groups=mesh['dp'=4,'section'=8,'tensor'=16] {'tensor'}, use_global_device_ids=true, to_apply=%region_1.3 | all-reduce | flops 384 | bytes 3072 | tf_op jit(solution)/shard_map/psum | solution.py:130
  297.9 3.9 collective-permute-done.5
  304.4 34.1 %all-gather.23.cloned.1.call-done = bf16[128,4096]{1,0:T(8,128)(2,1)} async-done(((bf16[128,256]{1,0:T(8,128)(2,1)}), bf16[128,4096]{1,0:T(8,128)(2,1)}) %all-gather.23.cloned.1.call-update) | async-done | bytes 1048592 | tf_op jit(solution)/shard_map/all_gather | solution.py:143
  338.5 3.3 convolution_convert_fusion.4
  346.3 51.2 %reduce-scatter.9.cloned.1.call-done = bf16[256,128]{0,1:T(8,128)(2,1)} async-done(((bf16[4096,128]{0,1:T(8,128)(2,1)}), bf16[256,128]{0,1:T(8,128)(2,1)}) %reduce-scatter.9.cloned.1.call-update) | async-done | bytes 65552 | tf_op jit(solution)/shard_map/reduce_scatter | solution.py:172
  403.4 5.4 collective-permute-start.6
  409.8 3.9 convolution_convert_fusion
  414.4 55.0 %reduce-scatter.11.cloned.1.call-done = bf16[256,128]{0,1:T(8,128)(2,1)} async-done(((bf16[4096,128]{0,1:T(8,128)(2,1)}), bf16[256,128]{0,1:T(8,128)(2,1)}) %reduce-scatter.11.cloned.1.call-update) | async-done | bytes 65552 | tf_op jit(solution)/shard_map/reduce_scatter | solution.py:211
  474.4 39.8 %all-gather.13.cloned.1.call-done = bf16[128,4096]{1,0:T(8,128)(2,1)} async-done(((bf16[128,256]{1,0:T(8,128)(2,1)}), bf16[128,4096]{1,0:T(8,128)(2,1)}) %all-gather.13.cloned.1.call-update) | async-done | bytes 1048592 | tf_op jit(solution)/shard_map/all_gather | solution.py:138
  514.1 3.3 convolution_convert_fusion.7
  518.5 40.8 %all-gather.15.cloned.1.call-done = bf16[128,4096]{0,1:T(8,128)(2,1)} async-done(((bf16[128,256]{0,1:T(8,128)(2,1)}), bf16[128,4096]{0,1:T(8,128)(2,1)}) %all-gather.15.cloned.1.call-update) | async-done | bytes 1048592 | tf_op jit(solution)/shard_map/all_gather | solution.py:164
  561.1 3.1 collective-permute-start.2
  567.0 24.6 %all-reduce = (f32[128]{0:T(128)}, f32[128]{0:T(128)}) all-reduce(f32[128]{0:T(128)} %get-tuple-element.37, f32[128]{0:T(128)} %get-tuple-element.28), channel_id=1, replica_groups=mesh['dp'=4,'section'=8,'tensor'=16] {'tensor'}, use_global_device_ids=true, to_apply=%region_4.7 | all-reduce | flops 256 | bytes 2048 | tf_op jit(solution)/shard_map/psum | solution.py:130
  594.8 42.7 %all-gather.17.cloned.1.call-done = bf16[128,4096]{1,0:T(8,128)(2,1)} async-done(((bf16[128,256]{1,0:T(8,128)(2,1)}), bf16[128,4096]{1,0:T(8,128)(2,1)}) %all-gather.17.cloned.1.call-update) | async-done | bytes 1048592 | tf_op jit(solution)/shard_map/all_gather | solution.py:138
  637.4 3.0 convolution_convert_fusion.6
  641.5 8.3 %psum.55 = f32[256]{0:T(256)S(1)} all-reduce(f32[256]{0:T(256)S(1)} %add.85), channel_id=1, replica_groups=mesh['dp'=4,'section'=8,'tensor'=16] {'dp'}, use_global_device_ids=true, to_apply=%region_24.27 | all-reduce | flops 256 | bytes 2048 | tf_op jit(solution)/shard_map/psum | solution.py:234
  650.4 31.9 %all-gather.19.cloned.1.call-done = bf16[128,4096]{0,1:T(8,128)(2,1)} async-done(((bf16[128,256]{0,1:T(8,128)(2,1)}), bf16[128,4096]{0,1:T(8,128)(2,1)}) %all-gather.19.cloned.1.call-update) | async-done | bytes 1048592 | tf_op jit(solution)/shard_map/all_gather | solution.py:164
  682.3 2.5 fusion.35
  (140 shorter events, 52.2 us)
Async XLA Ops:
  7.2 206.3 %copy-start = (s32[2,4]{1,0:T(2,128)S(1)}, s32[2,4]{1,0:T(2,128)}, u32[]{:S(2)}) copy-start(s32[2,4]{1,0:T(2,128)} %param.28) | copy-start | bytes 100
  7.2 73.7 %all-gather.27.cloned.1.call-start = ((), (), s32[]{:S(2)}) async-start(), calls=%async_computation.15 | async-start | bytes 2621440 | tf_op jit(solution)/shard_map/all_gather | solution.py:88
  7.9 67.3 %copy-start.20 = (bf16[1,1,128,256]{3,2,1,0:T(8,128)(2,1)S(1)}, bf16[1,1,128,256]{3,2,1,0:T(8,128)(2,1)}, u32[]{:S(2)}) copy-start(bf16[1,1,128,256]{3,2,1,0:T(8,128)(2,1)} %param.21) | copy-start | bytes 196612
  7.9 68.6 %copy-start.18 = (s32[2,1,1,128]{3,2,1,0:T(1,128)S(1)}, s32[2,1,1,128]{3,2,1,0:T(1,128)}, u32[]{:S(2)}) copy-start(s32[2,1,1,128]{3,2,1,0:T(1,128)} %param.31) | copy-start | bytes 3076
  7.9 92.2 %all-gather.21.cloned.1.call-start = ((), (), s32[]{:S(2)}) async-start(), calls=%async_computation.8 | async-start | bytes 1114112 | tf_op jit(solution)/shard_map/all_gather | solution.py:143
  41.2 95.5 %all-gather.25.cloned.1.call-start = ((), (), s32[]{:S(2)}) async-start(), calls=%async_computation.14 | async-start | bytes 2621440 | tf_op jit(solution)/shard_map/all_gather | solution.py:85
  41.9 155.4 %reduce-scatter.5.cloned.1.call-start = ((), (), s32[]{:S(2)}) async-start(), calls=%async_computation.9 | async-start | bytes 1114112 | tf_op jit(solution)/shard_map/reduce_scatter | solution.py:172
  65.7 18.6 %collective-permute-start.1 = (bf16[2,4096,64]{1,2,0:T(8,128)(2,1)S(1)}, bf16[2,4096,64]{1,2,0:T(8,128)(2,1)S(1)}, u32[]{:S(2)}, u32[]{:S(2)}) collective-permute-start(bf16[2,4096,64]{1,2,0:T(8,128)(2,1)S(1)} %constant_dynamic-update-slice_fusion), channel_id=1, source_target_pairs={{0,1},{1,0},{2,3},{3,2},{4,5},{5,4},{6,7},{7,6},{8,9},{9,8},{10,11... | collective-permute-start | bytes 3145736 | tf_op jit(solution)/shard_map/ppermute | solution.py:25
  75.3 5.6 collective-permute-start.3
  84.3 181.5 %reduce-scatter.7.cloned.1.call-start = ((), (), s32[]{:S(2)}) async-start(), calls=%async_computation.10 | async-start | bytes 1114112 | tf_op jit(solution)/shard_map/reduce_scatter | solution.py:211
  85.8 51.0 %copy-start.6 = (bf16[4096,128]{1,0:T(8,128)(2,1)}, bf16[4096,128]{1,0:T(8,128)(2,1)S(1)}, u32[]{:S(2)}) copy-start(bf16[4096,128]{1,0:T(8,128)(2,1)S(1)} %copy.17) | copy-start | bytes 3145732
  86.4 53.0 %copy-start.8 = (bf16[4096,128]{1,0:T(8,128)(2,1)}, bf16[4096,128]{1,0:T(8,128)(2,1)S(1)}, u32[]{:S(2)}) copy-start(bf16[4096,128]{1,0:T(8,128)(2,1)S(1)} %copy.18) | copy-start | bytes 3145732
  140.1 66.0 %copy-start.3 = (bf16[4096,64]{1,0:T(8,128)(2,1)S(1)}, bf16[4096,64]{1,0:T(8,128)(2,1)}, u32[]{:S(2)}) copy-start(bf16[4096,64]{1,0:T(8,128)(2,1)} %copy.25) | copy-start | bytes 1572868
  140.1 66.0 %copy-start.4 = (bf16[4096,64]{1,0:T(8,128)(2,1)S(1)}, bf16[4096,64]{1,0:T(8,128)(2,1)}, u32[]{:S(2)}) copy-start(bf16[4096,64]{1,0:T(8,128)(2,1)} %copy.26) | copy-start | bytes 1572868
  199.6 6.4 collective-permute-start.4
  210.1 55.7 %copy-start.2 = (bf16[2,1,1,128,256]{4,3,2,1,0:T(8,128)(2,1)S(1)}, bf16[2,1,1,128,256]{4,3,2,1,0:T(8,128)(2,1)}, u32[]{:S(2)}) copy-start(bf16[2,1,1,128,256]{4,3,2,1,0:T(8,128)(2,1)} %param.20) | copy-start | bytes 393220
  210.1 55.7 %copy-start.13 = (f32[1,256]{1,0:T(1,128)S(1)}, f32[1,256]{1,0:T(1,128)}, u32[]{:S(2)}) copy-start(f32[1,256]{1,0:T(1,128)} %param.23) | copy-start | bytes 3076
  210.1 91.8 %copy-start.1 = (bf16[1,4096,256]{2,1,0:T(8,128)(2,1)S(1)}, bf16[1,4096,256]{2,1,0:T(8,128)(2,1)}, u32[]{:S(2)}) copy-start(bf16[1,4096,256]{2,1,0:T(8,128)(2,1)} %all-gather.27.cloned.1.call-done) | copy-start | bytes 6291460
  210.1 128.4 %all-gather.23.cloned.1.call-start = ((), (), s32[]{:S(2)}) async-start(), calls=%async_computation.11 | async-start | bytes 1114112 | tf_op jit(solution)/shard_map/all_gather | solution.py:143
  210.2 18.0 %collective-permute-start = (bf16[1,128,256]{2,1,0:T(8,128)(2,1)}, bf16[1,128,256]{2,1,0:T(8,128)(2,1)S(1)}, u32[]{:S(2)}, u32[]{:S(2)}) collective-permute-start(bf16[1,128,256]{2,1,0:T(8,128)(2,1)} %bitcast.365), channel_id=1, source_target_pairs={{0,16},{16,32},{32,48},{48,64},{64,80},{80,96},{96,112},{1,17},{17... | collective-permute-start | bytes 196616 | tf_op jit(solution)/shard_map/ppermute | solution.py:31
  296.6 100.9 %reduce-scatter.9.cloned.1.call-start = ((), (), s32[]{:S(2)}) async-start(), calls=%async_computation.12 | async-start | bytes 1114112 | tf_op jit(solution)/shard_map/reduce_scatter | solution.py:172
  296.6 5.2 collective-permute-start.5
  303.7 165.7 %reduce-scatter.11.cloned.1.call-start = ((), (), s32[]{:S(2)}) async-start(), calls=%async_computation.13 | async-start | bytes 1114112 | tf_op jit(solution)/shard_map/reduce_scatter | solution.py:211
  403.4 6.4 collective-permute-start.6
  409.8 63.6 %copy-start.17 = (s32[2,4,128]{2,1,0:T(4,128)S(1)}, s32[2,4,128]{2,1,0:T(4,128)}, u32[]{:S(2)}) copy-start(s32[2,4,128]{2,1,0:T(4,128)} %param.29) | copy-start | bytes 12292
  413.8 100.3 %all-gather.13.cloned.1.call-start = ((), (), s32[]{:S(2)}) async-start(), calls=%async_computation.4 | async-start | bytes 1114112 | tf_op jit(solution)/shard_map/all_gather | solution.py:138
  471.6 87.7 %all-gather.15.cloned.1.call-start = ((), (), s32[]{:S(2)}) async-start(), calls=%async_computation.5 | async-start | bytes 1114112 | tf_op jit(solution)/shard_map/all_gather | solution.py:164
  518.4 119.0 %copy-start.7 = (bf16[4096,128]{1,0:T(8,128)(2,1)S(1)}, bf16[4096,128]{1,0:T(8,128)(2,1)}, u32[]{:S(2)}) copy-start(bf16[4096,128]{1,0:T(8,128)(2,1)} %copy-done.6) | copy-start | bytes 3145732
  518.5 119.0 %all-gather.17.cloned.1.call-start = ((), (), s32[]{:S(2)}) async-start(), calls=%async_computation.6 | async-start | bytes 1114112 | tf_op jit(solution)/shard_map/all_gather | solution.py:138
  561.1 4.4 collective-permute-start.2
  594.6 87.7 %all-gather.19.cloned.1.call-start = ((), (), s32[]{:S(2)}) async-start(), calls=%async_computation.7 | async-start | bytes 1114112 | tf_op jit(solution)/shard_map/all_gather | solution.py:164
  594.8 46.7 %copy-start.15 = (f32[256]{0:T(256)S(1)}, f32[256]{0:T(256)}, u32[]{:S(2)}) copy-start(f32[256]{0:T(256)} %get-tuple-element.29) | copy-start | bytes 3076
  (8 other events, 84.1 us)
Sparse Core Ops, SparseCore 0:
  10.1 43.6 all-gather.26
  56.4 43.6 all-gather.20
  102.2 34.4 all-gather.24
  139.4 57.9 reduce-scatter.4
  210.2 55.5 reduce-scatter.6
  296.7 41.7 all-gather.22
  341.3 56.1 reduce-scatter.8
  413.9 55.4 reduce-scatter.10
  472.0 42.0 all-gather.12
  518.6 40.6 all-gather.14
  594.7 42.6 all-gather.16
  641.6 40.6 all-gather.18
where the time goes:
time: 693 us; the launch traced here: 692 us
  waiting for transfers between devices  446 us (64%)
  blocking collectives  126 us (18%)
  matrix products  40.7 us (6%)
  starting transfers between devices  29.8 us (4%)
  between operations  18.6 us (3%)
  other arithmetic  17.6 us (3%)
  local copies, waits for them, and re-layouts  13.1 us (2%)
    reduce_scatter x2, waiting for transfers between devices, local(): lax.psum_scatter(lax.dot_general(out_w, grad_in, (((1,), (1,)), ((), ()))...  107 us
    reduce_scatter x2, waiting for transfers between devices, local(): lax.psum_scatter(lax.dot_general(grad_weights, grad_rows, (((1,), (1,)),...  91.8 us
    all_gather x2, waiting for transfers between devices, local(): lax.all_gather(forward_normed, 'tensor', axis=1, tiled=True)  82.4 us
    psum x3, blocking collectives, local(): lax.psum((jnp.sum(forward_f * forward_f, -1), jnp.sum(backward_f * backwa...  82.1 us
    all_gather x2, waiting for transfers between devices, local(): lax.all_gather(mixed, 'tensor', axis=1, tiled=True)  72.7 us
    all_gather x2, waiting for transfers between devices, local(): lax.all_gather(backward_normed, 'tensor', axis=1, tiled=True)  47.7 us
    all_gather x1, waiting for transfers between devices, local(): lax.all_gather(query_weight[0], 'dp', axis=0, tiled=True)  36.6 us
    ppermute x3, starting transfers between devices, partner_2(): return lax.ppermute(block, axis, route)  20.4 us
  transfers between devices with their start and end apart: 19, of which 14 were waited for; matrix products, arithmetic and copies ran while one was open for 4% of the time, Pallas kernels for 0%

commit v1 on v0

v1 whole, which is shorter than its diff:
```python
import math

import jax
import jax.numpy as jnp
from jax import lax
from jax.experimental import pallas as pl
from jax.experimental.pallas import tpu as pltpu
from jax.sharding import PartitionSpec as P

MODEL_WIDTH = 4096
HEAD = 128
TICKS = 2
ROWS = 128
BLK = 256
REPLICAS = 4
SECTIONS = 8
RING = 8
TENSOR = 16
SHARD = MODEL_WIDTH // REPLICAS
HALF = SHARD // 2
EPS = 1e-05
SCALE = HEAD ** (-0.5)
SEMS = 256
MESH = pl.DeviceIdType.MESH
F32 = jnp.float32
BF16 = jnp.bfloat16

S0, S1, F0, M0, F1, M1 = range(6)


def dot_nn(a, b):
    return lax.dot_general(a, b, (((1,), (0,)), ((), ())), preferred_element_type=F32)


def dot_nt(a, b):
    return lax.dot_general(a, b, (((1,), (1,)), ((), ())), preferred_element_type=F32)


def dot_tn(a, b):
    return lax.dot_general(a, b, (((0,), (0,)), ((), ())), preferred_element_type=F32)


def kernel(
    arrivals,
    fresh,
    stash,
    returning,
    loss_grad,
    gain,
    query_weight,
    key_weight,
    value_weight,
    w_out,
    plan,
    fresh_docs,
    arrival_docs,
    stash_docs,
    out_forward,
    out_backward,
    out_gain,
    wq,
    kv,
    ow,
    gath,
    gains,
    fr,
    yrecv,
    ysend,
    grad_in,
    masks,
    proj,
    proj_acc,
    inv_buf,
    part,
    part_sib,
    recv_sib,
    relay,
    relay_half,
    final,
    head_grad,
    grads,
    row_part,
    row_sib,
    row_all,
    gain_all,
    ss,
    rs,
    ls,
):
    d = lax.axis_index("dp")
    s = lax.axis_index("section")
    t = lax.axis_index("tensor")
    z = t // 2
    c = t % 2

    def zdev(k):
        return (d, s, lax.rem(t + 2 * k + TENSOR, TENSOR))

    sibling = (d, s, t + 1 - 2 * c)

    def xdev(k):
        return (lax.rem(d + k + REPLICAS, REPLICAS), s, t)

    def ydev(k):
        return (d, lax.rem(s + k + SECTIONS, SECTIONS), t)

    sends = []
    counter = [0]

    def new_id():
        counter[0] += 1
        return counter[0] - 1

    def describe(src, dst, i, device):
        return pltpu.make_async_remote_copy(
            src_ref=src,
            dst_ref=dst,
            send_sem=ss.at[i],
            recv_sem=rs.at[i],
            device_id=device,
            device_id_type=MESH,
        )

    def send(src, dst, device, keep=True):
        i = new_id()
        copy = describe(src, dst, i, device)
        copy.start()
        if keep:
            sends.append(copy)
            return i
        return (i, copy)

    def arrive(i, dst):
        describe(dst, dst, i, sibling).wait_recv()

    own = pl.ds(pl.multiple_of(d * SHARD, SHARD), SHARD)
    load_ow = pltpu.make_async_copy(w_out.at[0], ow.at[own], ls.at[0])
    load_wq = pltpu.make_async_copy(query_weight.at[0], wq.at[own], ls.at[1])
    load_ow.start()
    load_wq.start()
    kv[c, own, :] = jnp.concatenate([key_weight[0], value_weight[0]], axis=-1)

    peers = [zdev(k) for k in range(1, RING)] + [sibling]
    peers += [xdev(k) for k in range(1, REPLICAS)] + [ydev(1), ydev(-1)]
    barrier = pltpu.get_barrier_semaphore()
    for peer in peers:
        pl.semaphore_signal(barrier, inc=1, device_id=peer, device_id_type=MESH)
    pl.semaphore_wait(barrier, len(peers))

    def rows_of(k, half):
        base = lax.rem(d + k + REPLICAS, REPLICAS) * SHARD + half * HALF
        return pl.ds(pl.multiple_of(base, HALF), HALF)

    class Gather:
        def __init__(self, buffer, source):
            self.buffer = buffer
            self.source = source

        def start(self):
            b, src = self.buffer, self.source
            first, second = pl.ds(0, HALF), pl.ds(HALF, HALF)
            self.ids = [
                send(src.at[first], b.at[rows_of(0, 0)], xdev(1)),
                send(src.at[second], b.at[rows_of(0, 1)], xdev(-1)),
                send(src.at[second], b.at[rows_of(0, 1)], xdev(1)),
                send(src.at[first], b.at[rows_of(0, 0)], xdev(-1)),
            ]

        def forward(self):
            b = self.buffer
            arrive(self.ids[0], b.at[rows_of(-1, 0)])
            low = send(b.at[rows_of(-1, 0)], b.at[rows_of(-1, 0)], xdev(1))
            arrive(self.ids[1], b.at[rows_of(1, 1)])
            high = send(b.at[rows_of(1, 1)], b.at[rows_of(1, 1)], xdev(-1))
            self.ids += [low, high]

        def near(self):
            b = self.buffer
            arrive(self.ids[2], b.at[rows_of(-1, 1)])
            arrive(self.ids[3], b.at[rows_of(1, 0)])

        def far(self):
            b = self.buffer
            arrive(self.ids[4], b.at[rows_of(2, 0)])
            arrive(self.ids[5], b.at[rows_of(2, 1)])

    gather_ow = Gather(ow, w_out.at[0])
    gather_wq = Gather(wq, query_weight.at[0])
    gather_kv = Gather(kv.at[c], kv.at[c, own])

    gather_ow.start()

    y_forward = send(arrivals.at[0, 0], yrecv.at[0], ydev(1))
    y_backward = send(returning.at[0, 0], yrecv.at[1], ydev(-1))

    class AllGather:
        def __init__(self, buffer, half):
            self.b = buffer
            self.half = half

        def start(self):
            b = self.b
            src = b.at[c, 0]
            self.i3 = send(src, b.at[c, 3], zdev(2))
            self.i4 = send(src, b.at[c, 4], zdev(-2))
            self.i1 = send(src, b.at[c, 1], zdev(1))
            self.i2 = send(src, b.at[c, 2], zdev(-1))
            self.k0 = send(src, b.at[c, 0], sibling)

        def middle(self):
            b, h = self.b, self.half
            low, high = pl.ds(0, h), pl.ds(h, h)
            arrive(self.i3, b.at[c, 3])
            self.i5 = send(b.at[c, 3], b.at[c, 5], zdev(1))
            self.i7a = send(b.at[c, 3, low], b.at[c, 7, low], zdev(2))
            arrive(self.i4, b.at[c, 4])
            self.i6 = send(b.at[c, 4], b.at[c, 6], zdev(-1))
            self.i7b = send(b.at[c, 4, high], b.at[c, 7, high], zdev(-2))
            arrive(self.i1, b.at[c, 1])
            arrive(self.i2, b.at[c, 2])
            near = pl.ds(1, 4)
            self.k1 = send(b.at[c, near], b.at[c, near], sibling)

        def finish(self):
            b, h = self.b, self.half
            low, high = pl.ds(0, h), pl.ds(h, h)
            o = 1 - c
            arrive(self.i5, b.at[c, 5])
            arrive(self.i6, b.at[c, 6])
            arrive(self.i7a, b.at[c, 7, low])
            arrive(self.i7b, b.at[c, 7, high])
            away = pl.ds(5, 3)
            self.k2 = send(b.at[c, away], b.at[c, away], sibling)
            arrive(self.k0, b.at[o, 0])
            arrive(self.k1, b.at[o, pl.ds(1, 4)])

        def last(self):
            arrive(self.k2, self.b.at[1 - c, pl.ds(5, 3)])

    ag = [AllGather(gath.at[i], ROWS // 2) for i in range(6)]
    ag_gain = AllGather(gains, 8)

    gath[S0, c, 0] = stash[0, 0, 0]
    gath[S1, c, 0] = stash[1, 0, 0]
    gains[c, 0] = jnp.broadcast_to(gain[...], (16, BLK))
    ag_gain.start()
    ag[S0].start()
    ag[S1].start()

    fresh_ids = [[new_id() for _ in range(3)] for _ in range(TICKS)]

    @pl.when(s == 0)
    def _():
        for k in range(TICKS):
            fr[k, d] = fresh[k, 0]
            for n in range(3):
                describe(fresh.at[k, 0], fr.at[k, d], fresh_ids[k][n], xdev(n + 1)).start()

    def fresh_rows(k):
        for n in range(3):
            source = lax.rem(d - n - 1 + REPLICAS, REPLICAS)
            arrive(fresh_ids[k][n], fr.at[k, source])
        total = jnp.zeros((ROWS, BLK), BF16)
        for p in range(REPLICAS):
            total = jnp.where(plan[k, d] == p, fr[k, p], total)
        return total

    def balanced(k):
        total = jnp.zeros((1, ROWS), jnp.int32)
        for p in range(REPLICAS):
            total = jnp.where(plan[k, d] == p, fresh_docs[k, pl.ds(p, 1), :], total)
        return total

    causal = lax.broadcasted_iota(jnp.int32, (ROWS, ROWS), 0) >= lax.broadcasted_iota(
        jnp.int32, (ROWS, ROWS), 1
    )

    def store_mask(index, docs):
        across = jnp.broadcast_to(docs.astype(F32), (ROWS, ROWS))
        allowed = jnp.logical_and(across == across.T, causal)
        masks[index] = jnp.where(allowed, 1.0, 0.0)

    store_mask(0, stash_docs[0, 0])
    store_mask(1, stash_docs[1, 0])
    first_docs = balanced(0)
    for k in range(TICKS):
        arrived = arrival_docs[jnp.maximum(s - k - 1, 0)]
        new = first_docs if k == 0 else jnp.where(s == 0, balanced(1), first_docs)
        store_mask(2 + k, jnp.where(s > k, arrived, new))

    arrive(y_backward, yrecv.at[1])
    grad_in[0] = jnp.where(s == SECTIONS - 1, loss_grad[0, 0], yrecv[1])
    arrive(y_forward, yrecv.at[0])

    @pl.when(s == 0)
    def _():
        gath[F0, c, 0] = fresh_rows(0)

    @pl.when(s != 0)
    def _():
        gath[F0, c, 0] = yrecv[0]

    ag[F0].start()
    ag_gain.middle()
    ag[S0].middle()
    ag[S1].middle()

    def block_rows(p, core):
        k = (p + 1) // 2
        off = k * (1 - 2 * (p % 2))
        block = lax.rem(z + off + RING, RING) * 2 + core
        return pl.ds(pl.multiple_of(block * BLK, BLK), BLK)

    class ReduceScatter:
        def __init__(self, n, term):
            self.n = n
            self.term = term

        def fill(self, buffer, core, low, high):
            n, term = self.n, self.term

            def body(p, carry):
                buffer[n, p] = term(block_rows(p, core)).astype(BF16)
                return carry

            lax.fori_loop(low, high, body, 0)

        def start(self):
            n = self.n
            away, near = pl.ds(5, 3), pl.ds(0, 5)
            self.fill(part_sib, 1 - c, 5, 8)
            self.k1 = send(part_sib.at[n, away], recv_sib.at[n, away], sibling)
            self.fill(part_sib, 1 - c, 0, 5)
            self.k0 = send(part_sib.at[n, near], recv_sib.at[n, near], sibling)
            self.fill(part, c, 5, 8)
            arrive(self.k1, recv_sib.at[n, away])
            for p in range(5, 8):
                self.add(p)
            low, high = pl.ds(0, ROWS // 2), pl.ds(ROWS // 2, ROWS // 2)
            self.ra = send(part.at[n, 5], relay.at[n, 0], zdev(-1))
            self.rb = send(part.at[n, 6], relay.at[n, 1], zdev(1))
            self.ha = send(part.at[n, 7, low], relay_half.at[n, 0], zdev(-2))
            self.hb = send(part.at[n, 7, high], relay_half.at[n, 1], zdev(2))
            self.fill(part, c, 0, 5)
            arrive(self.k0, recv_sib.at[n, near])
            for p in (1, 2):
                self.add(p)
            self.d0 = send(part.at[n, 1], final.at[n, 0], zdev(-1))
            self.d1 = send(part.at[n, 2], final.at[n, 1], zdev(1))

        def add(self, p):
            n = self.n
            part[n, p] = (part[n, p].astype(F32) + recv_sib[n, p].astype(F32)).astype(BF16)

        def middle(self):
            n = self.n
            h = ROWS // 2
            arrive(self.ra, relay.at[n, 0])
            arrive(self.ha, relay_half.at[n, 0])
            sum3 = part[n, 3].astype(F32) + recv_sib[n, 3].astype(F32) + relay[n, 0].astype(F32)
            part[n, 3, pl.ds(0, h)] = (sum3[:h] + relay_half[n, 0].astype(F32)).astype(BF16)
            part[n, 3, pl.ds(h, h)] = sum3[h:].astype(BF16)
            self.d2 = send(part.at[n, 3], final.at[n, 2], zdev(-2))
            arrive(self.rb, relay.at[n, 1])
            arrive(self.hb, relay_half.at[n, 1])
            sum4 = part[n, 4].astype(F32) + recv_sib[n, 4].astype(F32) + relay[n, 1].astype(F32)
            part[n, 4, pl.ds(0, h)] = sum4[:h].astype(BF16)
            part[n, 4, pl.ds(h, h)] = (sum4[h:] + relay_half[n, 1].astype(F32)).astype(BF16)
            self.d3 = send(part.at[n, 4], final.at[n, 3], zdev(2))

        def finish(self):
            n = self.n
            total = part[n, 0].astype(F32) + recv_sib[n, 0].astype(F32)
            for q, i in enumerate((self.d0, self.d1, self.d2, self.d3)):
                arrive(i, final.at[n, q])
                total = total + final[n, q].astype(F32)
            return total

    def head_term(k):
        def term(rows):
            return dot_nt(grad_in[k], ow[rows, :])

        return term

    def weight_block(rows):
        return jnp.concatenate([wq[rows, :], kv[0, rows, :], kv[1, rows, :]], axis=1)

    def normed_term(k):
        def term(rows):
            return dot_nt(grads[k], weight_block(rows))

        return term

    gather_ow.forward()
    gather_wq.start()
    gather_kv.start()
    kv_own = send(kv.at[c, own], kv.at[c, own], sibling)
    load_ow.wait()
    load_wq.wait()
    ag[F0].middle()
    ag_gain.finish()
    ag[S0].finish()
    ag[S1].finish()
    ag[F0].finish()
    gather_ow.near()
    gather_ow.far()
    rs0 = ReduceScatter(0, head_term(0))
    rs0.start()
    gather_wq.forward()
    rs0.middle()
    gather_kv.forward()
    for index in (S0, S1, F0):
        ag[index].last()
    ag_gain.last()
    head_grad[0] = rs0.finish().astype(BF16)

    gather_kv.near()
    kv_ids = []
    for k in (-1, 1):
        rows = pl.ds(
            pl.multiple_of(lax.rem(d + k + REPLICAS, REPLICAS) * SHARD, SHARD), SHARD
        )
        kv_ids.append(send(kv.at[c, rows], kv.at[c, rows], sibling))
    gather_wq.near()
    gather_wq.far()
    gather_kv.far()
    rows = pl.ds(pl.multiple_of(lax.rem(d + 2, REPLICAS) * SHARD, SHARD), SHARD)
    kv_ids.append(send(kv.at[c, rows], kv.at[c, rows], sibling))
    arrive(kv_own, kv.at[1 - c, own])
    for i, k in zip(kv_ids, (-1, 1, 2)):
        rows = pl.ds(
            pl.multiple_of(lax.rem(d + k + REPLICAS, REPLICAS) * SHARD, SHARD), SHARD
        )
        arrive(i, kv.at[1 - c, rows])

    lane = lax.broadcasted_iota(jnp.int32, (ROWS, HEAD), 1)

    def project(indices, slots):
        count = len(indices)
        proj_acc[pl.ds(0, count * ROWS), :] = jnp.zeros((count * ROWS, 512), F32)

        def body(j, squares):
            p = j % RING
            core = j // RING
            g = gains[core, p, pl.ds(0, 1), :]
            pieces = []
            new = []
            for n, index in enumerate(indices):
                h = gath[index, core, p].astype(F32)
                sq = h * h
                new.append(squares[n] + sq[:, :HEAD] + sq[:, HEAD:])
                pieces.append((h * g).astype(BF16))
            lhs = pieces[0] if count == 1 else jnp.concatenate(pieces, axis=0)
            proj_acc[pl.ds(0, count * ROWS), :] += dot_nn(lhs, weight_block(block_rows(p, core)))
            return tuple(new)

        zero = jnp.zeros((ROWS, HEAD), F32)
        squares = lax.fori_loop(0, TENSOR, body, (zero,) * count)
        for n, slot in enumerate(slots):
            total = jnp.sum(squares[n], axis=-1, keepdims=True)
            inv = lax.rsqrt(total / MODEL_WIDTH + EPS)
            inv_buf[slot] = jnp.broadcast_to(inv, (ROWS, HEAD))
            acc = proj_acc[pl.ds(n * ROWS, ROWS), :] * inv
            low = acc[:, 256:384]
            high = acc[:, 384:512]
            key = jnp.where(lane < 64, low, pltpu.roll(high, 64, 1))
            value = jnp.where(lane < 64, pltpu.roll(low, 64, 1), high)
            proj[slot, 0] = acc[:, :128].astype(BF16)
            proj[slot, 1] = acc[:, 128:256].astype(BF16)
            proj[slot, 2] = key.astype(BF16)
            proj[slot, 3] = value.astype(BF16)

    def attention(slot, mask):
        q2 = jnp.concatenate([proj[slot, 0], proj[slot, 1]], axis=0)
        scores = dot_nt(q2, proj[slot, 2]) * SCALE
        allowed = jnp.concatenate([masks[mask], masks[mask]], axis=0) > 0.0
        raised = jnp.where(allowed, jnp.exp(scores), 0.0)
        return q2, raised / jnp.sum(raised, axis=-1, keepdims=True)

    def forward_attention(slot, mask, index):
        _, probs = attention(slot, mask)
        mixed = dot_nn(probs.astype(BF16), proj[slot, 3]).astype(BF16)
        gath[index, c, 0] = jnp.concatenate([mixed[:ROWS], mixed[ROWS:]], axis=1)

    def backward_attention(slot, mask, k):
        q2, probs = attention(slot, mask)
        key, value = proj[slot, 2], proj[slot, 3]
        hg = head_grad[k]
        hg2 = jnp.concatenate([hg[:, :HEAD], hg[:, HEAD:]], axis=0)
        prob_grad = dot_nt(hg2, value)
        inner = jnp.sum(probs * prob_grad, axis=-1, keepdims=True)
        score_grad = (probs * (prob_grad - inner) * SCALE).astype(BF16)
        query_grad = dot_nn(score_grad, key).astype(BF16).astype(F32)
        key_grad = dot_tn(score_grad, q2).astype(BF16).astype(F32)
        value_grad = dot_tn(probs.astype(BF16), hg2).astype(BF16).astype(F32)
        qf = q2.astype(F32)
        products = query_grad[:ROWS] * qf[:ROWS] + query_grad[ROWS:] * qf[ROWS:]
        products = products + key_grad * key.astype(F32) + value_grad * value.astype(F32)
        row = jnp.sum(products.T, axis=0, keepdims=True)
        row_part[k] = jnp.broadcast_to(row, (8, ROWS))
        low = jnp.where(lane < 64, key_grad, pltpu.roll(value_grad, 64, 1))
        high = jnp.where(lane < 64, pltpu.roll(key_grad, 64, 1), value_grad)
        grads[k] = jnp.concatenate(
            [query_grad[:ROWS], query_grad[ROWS:], low, high], axis=1
        ).astype(BF16)

    class RowSum:
        def __init__(self, k):
            self.k = k

        def start(self):
            self.i = send(row_part.at[self.k], row_sib.at[self.k], sibling)

        def middle(self):
            k = self.k
            arrive(self.i, row_sib.at[k])
            row_all[k, 0] = row_part[k] + row_sib[k]
            self.ids = [
                send(row_all.at[k, 0], row_all.at[k, n], zdev(n)) for n in range(1, RING)
            ]

        def finish(self):
            k = self.k
            total = row_all[k, 0]
            for n in range(1, RING):
                arrive(self.ids[n - 1], row_all.at[k, n])
                total = total + row_all[k, n]
            return jnp.broadcast_to(total[:1], (ROWS, ROWS)).T

    def backward_result(k, normed_grad, row):
        h = stash[k, 0, 0].astype(F32)
        inv = inv_buf[k][:, :1]
        scaled = normed_grad * gain[...]
        factor = inv * inv * row[:, :1] * (1.0 / MODEL_WIDTH)
        result = grad_in[k].astype(F32) + inv * scaled - h * factor
        term = jnp.sum(normed_grad * (h * inv), axis=0, keepdims=True)
        return result.astype(BF16), term

    def output_projection(index, hidden):
        def body(j, acc):
            p = j % RING
            core = j // RING
            return acc + dot_nn(gath[index, core, p], ow[block_rows(p, core), :])

        acc = lax.fori_loop(0, TENSOR, body, hidden.astype(F32))
        return acc.astype(BF16)

    project((S0, S1, F0), (0, 1, 2))
    backward_attention(0, 0, 0)
    rows0 = RowSum(0)
    rows0.start()
    rs1 = ReduceScatter(1, normed_term(0))
    rs1.start()
    rows0.middle()
    forward_attention(2, 2, M0)
    ag[M0].start()
    rs1.middle()
    ag[M0].middle()
    normed_grad = rs1.finish()
    result, gain_term0 = backward_result(0, normed_grad, rows0.finish())
    ysend[1] = result
    y_backward = send(ysend.at[1], yrecv.at[3], ydev(-1))
    ag[M0].finish()
    ag[M0].last()
    ysend[0] = output_projection(M0, gath[F0, c, 0])
    y_forward = send(ysend.at[0], yrecv.at[2], ydev(1))

    arrive(y_backward, yrecv.at[3])
    grad_in[1] = jnp.where(s == SECTIONS - 1, loss_grad[1, 0], yrecv[3])
    rs2 = ReduceScatter(2, head_term(1))
    rs2.start()
    arrive(y_forward, yrecv.at[2])

    @pl.when(s == 0)
    def _():
        gath[F1, c, 0] = fresh_rows(1)

    @pl.when(s != 0)
    def _():
        gath[F1, c, 0] = yrecv[2]

    ag[F1].start()
    rs2.middle()
    ag[F1].middle()
    head_grad[1] = rs2.finish().astype(BF16)
    backward_attention(1, 1, 1)
    rows1 = RowSum(1)
    rows1.start()
    rs3 = ReduceScatter(3, normed_term(1))
    rs3.start()
    rows1.middle()
    ag[F1].finish()
    ag[F1].last()
    project((F1,), (3,))
    forward_attention(3, 3, M1)
    ag[M1].start()
    rs3.middle()
    ag[M1].middle()
    normed_grad = rs3.finish()
    result, gain_term1 = backward_result(1, normed_grad, rows1.finish())
    out_backward[0, 0] = result
    gain_all[0] = jnp.broadcast_to(gain_term0 + gain_term1, (8, BLK))
    gain_ids = [send(gain_all.at[0], gain_all.at[n], xdev(n)) for n in range(1, REPLICAS)]
    ag[M1].finish()
    ag[M1].last()
    out_forward[0, 0] = output_projection(M1, gath[F1, c, 0])
    total = gain_all[0]
    for n in range(1, REPLICAS):
        arrive(gain_ids[n - 1], gain_all.at[n])
        total = total + gain_all[n]
    out_gain[...] = total[:1] * (1.0 / math.sqrt(TICKS * REPLICAS * ROWS))

    for copy in sends:
        copy.wait_send()

    @pl.when(s == 0)
    def _():
        for k in range(TICKS):
            for n in range(3):
                describe(fresh.at[k, 0], fr.at[k, d], fresh_ids[k][n], xdev(n + 1)).wait_send()


def local(*arguments):
    vmem = pl.BlockSpec(memory_space=pltpu.VMEM)
    anywhere = pl.BlockSpec(memory_space=pl.ANY)
    smem = pl.BlockSpec(memory_space=pltpu.SMEM)
    in_specs = [vmem] * 6 + [anywhere, vmem, vmem, anywhere, smem, vmem, vmem, vmem]
    block = (ROWS, BLK)
    scratch = [
        pltpu.VMEM((MODEL_WIDTH, BLK), BF16),
        pltpu.VMEM((2, MODEL_WIDTH, HEAD), BF16),
        pltpu.VMEM((MODEL_WIDTH, BLK), BF16),
        pltpu.VMEM((6, 2, RING) + block, BF16),
        pltpu.VMEM((2, RING, 16, BLK), F32),
        pltpu.VMEM((TICKS, REPLICAS) + block, BF16),
        pltpu.VMEM((4,) + block, BF16),
        pltpu.VMEM((2,) + block, BF16),
        pltpu.VMEM((TICKS,) + block, BF16),
        pltpu.VMEM((4, ROWS, ROWS), F32),
        pltpu.VMEM((4, 4, ROWS, HEAD), BF16),
        pltpu.VMEM((3 * ROWS, 512), F32),
        pltpu.VMEM((4, ROWS, HEAD), F32),
        pltpu.VMEM((4, RING) + block, BF16),
        pltpu.VMEM((4, RING) + block, BF16),
        pltpu.VMEM((4, RING) + block, BF16),
        pltpu.VMEM((4, 2) + block, BF16),
        pltpu.VMEM((4, 2, ROWS // 2, BLK), BF16),
        pltpu.VMEM((4, 4) + block, BF16),
        pltpu.VMEM((TICKS,) + block, BF16),
        pltpu.VMEM((TICKS, ROWS, 512), BF16),
        pltpu.VMEM((TICKS, 8, ROWS), F32),
        pltpu.VMEM((TICKS, 8, ROWS), F32),
        pltpu.VMEM((TICKS, RING, 8, ROWS), F32),
        pltpu.VMEM((REPLICAS, 8, BLK), F32),
        pltpu.SemaphoreType.DMA((SEMS,)),
        pltpu.SemaphoreType.DMA((SEMS,)),
        pltpu.SemaphoreType.DMA((2,)),
    ]
    return pl.pallas_call(
        kernel,
        out_shape=(
            jax.ShapeDtypeStruct((1, 1) + block, BF16),
            jax.ShapeDtypeStruct((1, 1) + block, BF16),
            jax.ShapeDtypeStruct((1, BLK), F32),
        ),
        in_specs=in_specs,
        out_specs=(vmem, vmem, vmem),
        scratch_shapes=scratch,
        compiler_params=pltpu.CompilerParams(
            collective_id=0, has_side_effects=True, vmem_limit_bytes=56 << 20
        ),
    )(*arguments)


def solution(mesh):
    return jax.shard_map(
        local,
        mesh=mesh,
        in_specs=(
            P("section", "dp", None, "tensor"),
            P(None, "dp", None, "tensor"),
            P(None, "section", "dp", None, "tensor"),
            P("section", "dp", None, "tensor"),
            P(None, "dp", None, "tensor"),
            P("section", "tensor"),
            P("section", "dp", "tensor"),
            P("section", "dp", "tensor"),
            P("section", "dp", "tensor"),
            P("section", "dp", "tensor"),
            P(),
            P(),
            P(None, "dp", None),
            P(None, "section", "dp", None),
        ),
        out_specs=(
            P("section", "dp", None, "tensor"),
            P("section", "dp", None, "tensor"),
            P("section", "tensor"),
        ),
        check_vma=False,
    )
```

time: 693 us -> 149 us (0.22)
  waiting for transfers between devices: 446 us -> 0 us
  Pallas kernels: 0 us -> 143 us
  blocking collectives: 126 us -> 0 us
  matrix products: 40.7 us -> 0 us
  starting transfers between devices: 29.8 us -> 0 us
  between operations: 18.6 us -> 0.66 us
  other arithmetic: 17.6 us -> 0 us
  local copies, waits for them, and re-layouts: 13.1 us -> 5.31 us
    all_gather x8 -> x0, waiting for transfers between devices: 239 us -> none  [the longest x2 82.4 us: local(): lax.all_gather(forward_normed, 'tensor', axis=1, tiled=True)]
    reduce_scatter x4 -> x0, waiting for transfers between devices: 199 us -> none  [the longest x2 107 us: local(): lax.psum_scatter(lax.dot_general(out_w, grad_in, (((1,), (1,)), ((), ()))...]
    pallas_call x0 -> x1, Pallas kernels: none -> 143 us  [local(): pl.pallas_call(kernel, out_shape=(jax.ShapeDtypeStruct((1, 1) + block, BF...]
    psum x4 -> x0, blocking collectives: 90.4 us -> none  [the longest x3 82.1 us: local(): lax.psum((jnp.sum(forward_f * forward_f, -1), jnp.sum(backward_f * backwa...]
    dot_general x24 -> x0, matrix products: 40.7 us -> none  [the longest x2 7.92 us: local(): lax.dot_general(grad_weights, grad_rows, (((1,), (1,)), ((), ())), prefer...]
    all_gather x3 -> x0, blocking collectives: 35.1 us -> none  [the longest x1 12.9 us: local(): lax.all_gather(key_weight[0], 'dp', axis=0, tiled=True)]
    ppermute x7 -> x0, starting transfers between devices: 29.3 us -> none  [the longest x3 20.4 us: partner_2(): return lax.ppermute(block, axis, route)]
  transfers between devices with their start and end apart: 19 -> 0, of which waited for: 14 -> 0; matrix products, arithmetic and copies ran while one was open for 4% -> 0% of each run, Pallas kernels for 0% -> 0%
where the time goes in v1:
time: 149 us
  Pallas kernels  143 us (96%)
  local copies, waits for them, and re-layouts  5.31 us (4%)
    pallas_call x1, Pallas kernels, local(): pl.pallas_call(kernel, out_shape=(jax.ShapeDtypeStruct((1, 1) + block, BF...  143 us
    unnamed x11, local copies, waits for them, and re-layouts  5.31 us

profile of v1, /device:TPU:1, one launch (start us, length us, event | category | flops | bytes accessed | tf_op | source)
XLA Modules:
  0.0 149.0 jit_solution(13127385618658167849)
XLA Ops:
  0.6 0.0 copy-start
  0.6 1.8 %copy.17.key_weight = bf16[1,1024,64]{2,1,0:T(8,128)(2,1)} copy(bf16[1,1024,64]{1,2,0:T(8,128)(2,1)} %param.21) | data formatting | bytes 262144 | tf_op args[7]
  2.4 0.0 copy-done
  2.4 0.8 copy.18.value_weight
  3.2 143.0 %shard_map.157 = (bf16[1,1,128,256]{3,2,1,0:T(8,128)(2,1)}, bf16[1,1,128,256]{3,2,1,0:T(8,128)(2,1)}, f32[1,256]{1,0:T(1,128)}) custom-call(bf16[1,1,128,256]{3,2,1,0:T(8,128)(2,1)} %arrivals.1, bf16[2,1,128,256]{3,2,1,0:T(8,128)(2,1)} %fresh.1, bf16[2,1,1,128,256]{4,3,2,1,0:T(8,128)(2,1)} %stash.1, bf16[1,1,128,256]{3,2,1,0:T(8,128)(2,1)} %returning.1, ...), custom_call_target="tpu_custom_call" | custom-call | tf_op jit(solution)/shard_map/pallas_call | solution.py:659
  146.2 0.0 copy-start.1
  146.3 1.5 %copy.22 = bf16[1,1,128,256]{3,2,1,0:T(8,128)(2,1)} copy(bf16[1,1,128,256]{3,2,1,0:T(8,128)(2,1)} %get-tuple-element.6) | data formatting | bytes 131072
  147.8 0.0 copy-done.1
  147.8 0.0 copy-start.2
  147.8 0.6 copy.23
  148.4 0.0 copy-done.2
  148.4 0.6 copy.24
Async XLA Ops:
  0.6 1.8 %copy-start = (bf16[1,1024,64]{1,2,0:T(8,128)(2,1)S(1)}, bf16[1,1024,64]{1,2,0:T(8,128)(2,1)}, u32[]{:S(2)}) copy-start(bf16[1,1024,64]{1,2,0:T(8,128)(2,1)} %param.22) | copy-start | bytes 393220
  146.2 1.5 %copy-start.1 = (bf16[1,1,128,256]{3,2,1,0:T(8,128)(2,1)S(1)}, bf16[1,1,128,256]{3,2,1,0:T(8,128)(2,1)}, u32[]{:S(2)}) copy-start(bf16[1,1,128,256]{3,2,1,0:T(8,128)(2,1)} %get-tuple-element.7) | copy-start | bytes 196612
  147.8 0.6 copy-start.2

commit v2 on v1

--- a/solution.py
+++ b/solution.py
@@ -136,9 +136,10 @@
     own = pl.ds(pl.multiple_of(d * SHARD, SHARD), SHARD)
     load_ow = pltpu.make_async_copy(w_out.at[0], ow.at[own], ls.at[0])
     load_wq = pltpu.make_async_copy(query_weight.at[0], wq.at[own], ls.at[1])
-    load_ow.start()
-    load_wq.start()
-    kv[c, own, :] = jnp.concatenate([key_weight[0], value_weight[0]], axis=-1)
+    load_key = pltpu.make_async_copy(key_weight.at[0], kv.at[c, d, pl.ds(0, 64)], ls.at[2])
+    load_value = pltpu.make_async_copy(value_weight.at[0], kv.at[c, d, pl.ds(64, 64)], ls.at[3])
+    for load in (load_key, load_value, load_wq, load_ow):
+        load.start()
 
     peers = [zdev(k) for k in range(1, RING)] + [sibling]
     peers += [xdev(k) for k in range(1, REPLICAS)] + [ydev(1), ydev(-1)]
@@ -147,46 +148,54 @@
         pl.semaphore_signal(barrier, inc=1, device_id=peer, device_id_type=MESH)
     pl.semaphore_wait(barrier, len(peers))
 
-    def rows_of(k, half):
-        base = lax.rem(d + k + REPLICAS, REPLICAS) * SHARD + half * HALF
-        return pl.ds(pl.multiple_of(base, HALF), HALF)
+    def replica(k):
+        return lax.rem(d + k + REPLICAS, REPLICAS)
+
+    def rows_at(buffer):
+        def at(k, half):
+            base = replica(k) * SHARD + half * HALF
+            return buffer.at[pl.ds(pl.multiple_of(base, HALF), HALF)]
+
+        return at
+
+    def kv_at(k, half):
+        return kv.at[c, replica(k), pl.ds(half * 64, 64)]
 
     class Gather:
-        def __init__(self, buffer, source):
-            self.buffer = buffer
-            self.source = source
+        def __init__(self, at, first, second):
+            self.at = at
+            self.first = first
+            self.second = second
 
         def start(self):
-            b, src = self.buffer, self.source
-            first, second = pl.ds(0, HALF), pl.ds(HALF, HALF)
+            at = self.at
             self.ids = [
-                send(src.at[first], b.at[rows_of(0, 0)], xdev(1)),
-                send(src.at[second], b.at[rows_of(0, 1)], xdev(-1)),
-                send(src.at[second], b.at[rows_of(0, 1)], xdev(1)),
-                send(src.at[first], b.at[rows_of(0, 0)], xdev(-1)),
+                send(self.first, at(0, 0), xdev(1)),
+                send(self.second, at(0, 1), xdev(-1)),
+                send(self.second, at(0, 1), xdev(1)),
+                send(self.first, at(0, 0), xdev(-1)),
             ]
 
         def forward(self):
-            b = self.buffer
-            arrive(self.ids[0], b.at[rows_of(-1, 0)])
-            low = send(b.at[rows_of(-1, 0)], b.at[rows_of(-1, 0)], xdev(1))
-            arrive(self.ids[1], b.at[rows_of(1, 1)])
-            high = send(b.at[rows_of(1, 1)], b.at[rows_of(1, 1)], xdev(-1))
+            at = self.at
+            arrive(self.ids[0], at(-1, 0))
+            low = send(at(-1, 0), at(-1, 0), xdev(1))
+            arrive(self.ids[1], at(1, 1))
+            high = send(at(1, 1), at(1, 1), xdev(-1))
             self.ids += [low, high]
 
         def near(self):
-            b = self.buffer
-            arrive(self.ids[2], b.at[rows_of(-1, 1)])
-            arrive(self.ids[3], b.at[rows_of(1, 0)])
+            arrive(self.ids[2], self.at(-1, 1))
+            arrive(self.ids[3], self.at(1, 0))
 
         def far(self):
-            b = self.buffer
-            arrive(self.ids[4], b.at[rows_of(2, 0)])
-            arrive(self.ids[5], b.at[rows_of(2, 1)])
-
-    gather_ow = Gather(ow, w_out.at[0])
-    gather_wq = Gather(wq, query_weight.at[0])
-    gather_kv = Gather(kv.at[c], kv.at[c, own])
+            arrive(self.ids[4], self.at(2, 0))
+            arrive(self.ids[5], self.at(2, 1))
+
+    first, second = pl.ds(0, HALF), pl.ds(HALF, HALF)
+    gather_ow = Gather(rows_at(ow), w_out.at[0, first], w_out.at[0, second])
+    gather_wq = Gather(rows_at(wq), query_weight.at[0, first], query_weight.at[0, second])
+    gather_kv = Gather(kv_at, key_weight.at[0], value_weight.at[0])
 
     gather_ow.start()
 
@@ -305,10 +314,16 @@
     ag[S0].middle()
     ag[S1].middle()
 
-    def block_rows(p, core):
+    def block_of(p, core):
         k = (p + 1) // 2
         off = k * (1 - 2 * (p % 2))
-        block = lax.rem(z + off + RING, RING) * 2 + core
+        return lax.rem(z + off + RING, RING) * 2 + core
+
+    def slot_of(block):
+        off = lax.rem(block // 2 - z + RING, RING)
+        return 2 * off + (off // 4) * (15 - 4 * off)
+
+    def rows_of(block):
         return pl.ds(pl.multiple_of(block * BLK, BLK), BLK)
 
     class ReduceScatter:
@@ -320,10 +335,10 @@
             n, term = self.n, self.term
 
             def body(p, carry):
-                buffer[n, p] = term(block_rows(p, core)).astype(BF16)
+                buffer[n, p] = term(block_of(p, core)).astype(BF16)
                 return carry
 
-            lax.fori_loop(low, high, body, 0)
+            lax.fori_loop(low, high, body, 0, unroll=high - low)
 
         def start(self):
             n = self.n
@@ -377,98 +392,92 @@
             return total
 
     def head_term(k):
-        def term(rows):
-            return dot_nt(grad_in[k], ow[rows, :])
+        def term(block):
+            return dot_nt(grad_in[k], ow[rows_of(block), :])
 
         return term
 
-    def weight_block(rows):
-        return jnp.concatenate([wq[rows, :], kv[0, rows, :], kv[1, rows, :]], axis=1)
+    def kv_block(block):
+        lanes = pl.ds(pl.multiple_of(lax.rem(block, 4) * BLK, BLK), BLK)
+        return jnp.concatenate([kv[0, block // 4, :, lanes], kv[1, block // 4, :, lanes]], axis=0)
 
     def normed_term(k):
-        def term(rows):
-            return dot_nt(grads[k], weight_block(rows))
+        def term(block):
+            query_part = dot_nt(grads[k, :, pl.ds(0, BLK)], wq[rows_of(block), :])
+            return query_part + dot_nn(grads[k, :, pl.ds(BLK, BLK)], kv_block(block))
 
         return term
 
     gather_ow.forward()
     gather_wq.start()
     gather_kv.start()
-    kv_own = send(kv.at[c, own], kv.at[c, own], sibling)
-    load_ow.wait()
-    load_wq.wait()
+    for load in (load_key, load_value, load_wq, load_ow):
+        load.wait()
+    kv_own = send(kv.at[c, d], kv.at[c, d], sibling)
     ag[F0].middle()
     ag_gain.finish()
     ag[S0].finish()
     ag[S1].finish()
     ag[F0].finish()
+    gather_wq.forward()
     gather_ow.near()
     gather_ow.far()
     rs0 = ReduceScatter(0, head_term(0))
     rs0.start()
-    gather_wq.forward()
+    gather_kv.forward()
     rs0.middle()
-    gather_kv.forward()
     for index in (S0, S1, F0):
         ag[index].last()
     ag_gain.last()
     head_grad[0] = rs0.finish().astype(BF16)
 
-    gather_kv.near()
-    kv_ids = []
-    for k in (-1, 1):
-        rows = pl.ds(
-            pl.multiple_of(lax.rem(d + k + REPLICAS, REPLICAS) * SHARD, SHARD), SHARD
-        )
-        kv_ids.append(send(kv.at[c, rows], kv.at[c, rows], sibling))
-    gather_wq.near()
-    gather_wq.far()
-    gather_kv.far()
-    rows = pl.ds(pl.multiple_of(lax.rem(d + 2, REPLICAS) * SHARD, SHARD), SHARD)
-    kv_ids.append(send(kv.at[c, rows], kv.at[c, rows], sibling))
-    arrive(kv_own, kv.at[1 - c, own])
-    for i, k in zip(kv_ids, (-1, 1, 2)):
-        rows = pl.ds(
-            pl.multiple_of(lax.rem(d + k + REPLICAS, REPLICAS) * SHARD, SHARD), SHARD
-        )
-        arrive(i, kv.at[1 - c, rows])
-
     lane = lax.broadcasted_iota(jnp.int32, (ROWS, HEAD), 1)
 
-    def project(indices, slots):
-        count = len(indices)
-        proj_acc[pl.ds(0, count * ROWS), :] = jnp.zeros((count * ROWS, 512), F32)
-
-        def body(j, squares):
-            p = j % RING
-            core = j // RING
-            g = gains[core, p, pl.ds(0, 1), :]
-            pieces = []
-            new = []
-            for n, index in enumerate(indices):
-                h = gath[index, core, p].astype(F32)
-                sq = h * h
-                new.append(squares[n] + sq[:, :HEAD] + sq[:, HEAD:])
-                pieces.append((h * g).astype(BF16))
-            lhs = pieces[0] if count == 1 else jnp.concatenate(pieces, axis=0)
-            proj_acc[pl.ds(0, count * ROWS), :] += dot_nn(lhs, weight_block(block_rows(p, core)))
-            return tuple(new)
-
-        zero = jnp.zeros((ROWS, HEAD), F32)
-        squares = lax.fori_loop(0, TENSOR, body, (zero,) * count)
-        for n, slot in enumerate(slots):
-            total = jnp.sum(squares[n], axis=-1, keepdims=True)
-            inv = lax.rsqrt(total / MODEL_WIDTH + EPS)
-            inv_buf[slot] = jnp.broadcast_to(inv, (ROWS, HEAD))
-            acc = proj_acc[pl.ds(n * ROWS, ROWS), :] * inv
-            low = acc[:, 256:384]
-            high = acc[:, 384:512]
-            key = jnp.where(lane < 64, low, pltpu.roll(high, 64, 1))
-            value = jnp.where(lane < 64, pltpu.roll(low, 64, 1), high)
-            proj[slot, 0] = acc[:, :128].astype(BF16)
-            proj[slot, 1] = acc[:, 128:256].astype(BF16)
-            proj[slot, 2] = key.astype(BF16)
-            proj[slot, 3] = value.astype(BF16)
+    class Project:
+        def __init__(self, indices, slots):
+            self.indices = indices
+            self.slots = slots
+            count = len(indices)
+            self.rows = pl.ds(0, count * ROWS)
+            proj_acc[self.rows, :] = jnp.zeros((count * ROWS, 512), F32)
+            self.squares = (jnp.zeros((ROWS, HEAD), F32),) * count
+
+        def add(self, owner):
+            rows = self.rows
+            squares = list(self.squares)
+            columns = []
+            for q in range(4):
+                block = owner * 4 + q
+                p, core = slot_of(block), q % 2
+                g = gains[core, p, pl.ds(0, 1), :]
+                pieces = []
+                for n, index in enumerate(self.indices):
+                    h = gath[index, core, p].astype(F32)
+                    sq = h * h
+                    squares[n] = squares[n] + sq[:, :HEAD] + sq[:, HEAD:]
+                    pieces.append((h * g).astype(BF16))
+                columns.append(jnp.concatenate(pieces, axis=0))
+            self.squares = squares
+            lhs = jnp.concatenate(columns, axis=1)
+            weight = wq[pl.ds(pl.multiple_of(owner * SHARD, SHARD), SHARD), :]
+            proj_acc[rows, pl.ds(0, BLK)] += dot_nn(lhs, weight)
+            both = jnp.concatenate([kv[0, owner], kv[1, owner]], axis=0)
+            proj_acc[rows, pl.ds(BLK, BLK)] += dot_nt(lhs, both)
+
+        def done(self):
+            for n, slot in enumerate(self.slots):
+                total = jnp.sum(self.squares[n], axis=-1, keepdims=True)
+                inv = lax.rsqrt(total / MODEL_WIDTH + EPS)
+                inv_buf[slot] = jnp.broadcast_to(inv, (ROWS, HEAD))
+                acc = proj_acc[pl.ds(n * ROWS, ROWS), :] * inv
+                low = acc[:, 256:384]
+                high = acc[:, 384:512]
+                key = jnp.where(lane < 64, low, pltpu.roll(high, 64, 1))
+                value = jnp.where(lane < 64, pltpu.roll(low, 64, 1), high)
+                proj[slot, 0] = acc[:, :128].astype(BF16)
+                proj[slot, 1] = acc[:, 128:256].astype(BF16)
+                proj[slot, 2] = key.astype(BF16)
+                proj[slot, 3] = value.astype(BF16)
 
     def attention(slot, mask):
         q2 = jnp.concatenate([proj[slot, 0], proj[slot, 1]], axis=0)
@@ -537,15 +546,29 @@
         return result.astype(BF16), term
 
     def output_projection(index, hidden):
-        def body(j, acc):
-            p = j % RING
-            core = j // RING
-            return acc + dot_nn(gath[index, core, p], ow[block_rows(p, core), :])
-
-        acc = lax.fori_loop(0, TENSOR, body, hidden.astype(F32))
+        acc = hidden.astype(F32)
+        for part_of in range(2):
+            blocks = range(part_of * 8, part_of * 8 + 8)
+            lhs = jnp.concatenate([gath[index, b % 2, slot_of(b)] for b in blocks], axis=1)
+            acc = acc + dot_nn(lhs, ow[pl.ds(part_of * 8 * BLK, 8 * BLK), :])
         return acc.astype(BF16)
 
-    project((S0, S1, F0), (0, 1, 2))
+    project = Project((S0, S1, F0), (0, 1, 2))
+    arrive(kv_own, kv.at[1 - c, d])
+    project.add(replica(0))
+    gather_kv.near()
+    kv_ids = [send(kv.at[c, replica(k)], kv.at[c, replica(k)], sibling) for k in (-1, 1)]
+    gather_wq.near()
+    for i, k in zip(kv_ids, (-1, 1)):
+        arrive(i, kv.at[1 - c, replica(k)])
+    project.add(replica(-1))
+    project.add(replica(1))
+    gather_kv.far()
+    kv_far = send(kv.at[c, replica(2)], kv.at[c, replica(2)], sibling)
+    gather_wq.far()
+    arrive(kv_far, kv.at[1 - c, replica(2)])
+    project.add(replica(2))
+    project.done()
     backward_attention(0, 0, 0)
     rows0 = RowSum(0)
     rows0.start()
@@ -591,7 +614,10 @@
     rows1.middle()
     ag[F1].finish()
     ag[F1].last()
-    project((F1,), (3,))
+    project = Project((F1,), (3,))
+    for owner in range(REPLICAS):
+        project.add(owner)
+    project.done()
     forward_attention(3, 3, M1)
     ag[M1].start()
     rs3.middle()
@@ -624,11 +650,14 @@
     vmem = pl.BlockSpec(memory_space=pltpu.VMEM)
     anywhere = pl.BlockSpec(memory_space=pl.ANY)
     smem = pl.BlockSpec(memory_space=pltpu.SMEM)
-    in_specs = [vmem] * 6 + [anywhere, vmem, vmem, anywhere, smem, vmem, vmem, vmem]
+    in_specs = [vmem] * 6 + [anywhere] * 4 + [smem, vmem, vmem, vmem]
+    arguments = list(arguments)
+    for n in (7, 8):
+        arguments[n] = jnp.swapaxes(arguments[n], 1, 2)
     block = (ROWS, BLK)
     scratch = [
         pltpu.VMEM((MODEL_WIDTH, BLK), BF16),
-        pltpu.VMEM((2, MODEL_WIDTH, HEAD), BF16),
+        pltpu.VMEM((2, REPLICAS, HEAD, SHARD), BF16),
         pltpu.VMEM((MODEL_WIDTH, BLK), BF16),
         pltpu.VMEM((6, 2, RING) + block, BF16),
         pltpu.VMEM((2, RING, 16, BLK), F32),
@@ -654,7 +683,7 @@
         pltpu.VMEM((REPLICAS, 8, BLK), F32),
         pltpu.SemaphoreType.DMA((SEMS,)),
         pltpu.SemaphoreType.DMA((SEMS,)),
-        pltpu.SemaphoreType.DMA((2,)),
+        pltpu.SemaphoreType.DMA((4,)),
     ]
     return pl.pallas_call(
         kernel,

time: 149 us -> 136 us (0.913)
  Pallas kernels: 143 us -> 132 us
  local copies, waits for them, and re-layouts: 5.31 us -> 2.71 us
    pallas_call x1, Pallas kernels: 143 us -> 132 us  [local(): pl.pallas_call(kernel, out_shape=(jax.ShapeDtypeStruct((1, 1) + block, BF...]
    unnamed x11 -> x7, local copies, waits for them, and re-layouts: 5.31 us -> 2.71 us
where the time goes in v2:
time: 136 us; the launch traced here: 135 us
  Pallas kernels  132 us (97%)
  local copies, waits for them, and re-layouts  2.71 us (2%)
    pallas_call x1, Pallas kernels, local(): pl.pallas_call(kernel, out_shape=(jax.ShapeDtypeStruct((1, 1) + block, BF...  132 us

profile of v2, /device:TPU:1, one launch (start us, length us, event | category | flops | bytes accessed | tf_op | source)
XLA Modules:
  0.0 135.4 jit_solution(6957322555084097950)
XLA Ops:
  0.6 132.0 %shard_map.157 = (bf16[1,1,128,256]{3,2,1,0:T(8,128)(2,1)}, bf16[1,1,128,256]{3,2,1,0:T(8,128)(2,1)}, f32[1,256]{1,0:T(1,128)}) custom-call(bf16[1,1,128,256]{3,2,1,0:T(8,128)(2,1)} %arrivals.1, bf16[2,1,128,256]{3,2,1,0:T(8,128)(2,1)} %fresh.1, bf16[2,1,1,128,256]{4,3,2,1,0:T(8,128)(2,1)} %stash.1, bf16[1,1,128,256]{3,2,1,0:T(8,128)(2,1)} %returning.1, ...), custom_call_target="tpu_custom_call" | custom-call | tf_op jit(solution)/shard_map/pallas_call | solution.py:688
  132.6 0.0 copy-start
  132.7 1.5 %copy.20 = bf16[1,1,128,256]{3,2,1,0:T(8,128)(2,1)} copy(bf16[1,1,128,256]{3,2,1,0:T(8,128)(2,1)} %get-tuple-element.6) | data formatting | bytes 131072
  134.2 0.0 copy-done
  134.2 0.0 copy-start.1
  134.2 0.6 copy.21
  134.8 0.0 copy-done.1
  134.8 0.6 copy.22
Async XLA Ops:
  132.6 1.5 %copy-start = (bf16[1,1,128,256]{3,2,1,0:T(8,128)(2,1)S(1)}, bf16[1,1,128,256]{3,2,1,0:T(8,128)(2,1)}, u32[]{:S(2)}) copy-start(bf16[1,1,128,256]{3,2,1,0:T(8,128)(2,1)} %get-tuple-element.7) | copy-start | bytes 196612
  134.2 0.6 copy-start.1

commit v3 on v2

--- a/solution.py
+++ b/solution.py
@@ -410,7 +410,6 @@
 
     gather_ow.forward()
     gather_wq.start()
-    gather_kv.start()
     for load in (load_key, load_value, load_wq, load_ow):
         load.wait()
     kv_own = send(kv.at[c, d], kv.at[c, d], sibling)
@@ -419,8 +418,9 @@
     ag[S0].finish()
     ag[S1].finish()
     ag[F0].finish()
+    gather_ow.near()
+    gather_kv.start()
     gather_wq.forward()
-    gather_ow.near()
     gather_ow.far()
     rs0 = ReduceScatter(0, head_term(0))
     rs0.start()
@@ -569,49 +569,42 @@
     arrive(kv_far, kv.at[1 - c, replica(2)])
     project.add(replica(2))
     project.done()
+    forward_attention(2, 2, M0)
+    ag[M0].start()
     backward_attention(0, 0, 0)
     rows0 = RowSum(0)
     rows0.start()
     rs1 = ReduceScatter(1, normed_term(0))
     rs1.start()
     rows0.middle()
-    forward_attention(2, 2, M0)
-    ag[M0].start()
+    ag[M0].middle()
     rs1.middle()
-    ag[M0].middle()
+    ag[M0].finish()
+    ag[M0].last()
+    ysend[0] = output_projection(M0, gath[F0, c, 0])
+    y_forward = send(ysend.at[0], yrecv.at[2], ydev(1))
     normed_grad = rs1.finish()
     result, gain_term0 = backward_result(0, normed_grad, rows0.finish())
     ysend[1] = result
     y_backward = send(ysend.at[1], yrecv.at[3], ydev(-1))
-    ag[M0].finish()
-    ag[M0].last()
-    ysend[0] = output_projection(M0, gath[F0, c, 0])
-    y_forward = send(ysend.at[0], yrecv.at[2], ydev(1))
-
+
+    arrive(y_forward, yrecv.at[2])
+
+    @pl.when(s == 0)
+    def _():
+        gath[F1, c, 0] = fresh_rows(1)
+
+    @pl.when(s != 0)
+    def _():
+        gath[F1, c, 0] = yrecv[2]
+
+    ag[F1].start()
     arrive(y_backward, yrecv.at[3])
     grad_in[1] = jnp.where(s == SECTIONS - 1, loss_grad[1, 0], yrecv[3])
     rs2 = ReduceScatter(2, head_term(1))
     rs2.start()
-    arrive(y_forward, yrecv.at[2])
-
-    @pl.when(s == 0)
-    def _():
-        gath[F1, c, 0] = fresh_rows(1)
-
-    @pl.when(s != 0)
-    def _():
-        gath[F1, c, 0] = yrecv[2]
-
-    ag[F1].start()
+    ag[F1].middle()
     rs2.middle()
-    ag[F1].middle()
-    head_grad[1] = rs2.finish().astype(BF16)
-    backward_attention(1, 1, 1)
-    rows1 = RowSum(1)
-    rows1.start()
-    rs3 = ReduceScatter(3, normed_term(1))
-    rs3.start()
-    rows1.middle()
     ag[F1].finish()
     ag[F1].last()
     project = Project((F1,), (3,))
@@ -620,16 +613,23 @@
     project.done()
     forward_attention(3, 3, M1)
     ag[M1].start()
+    head_grad[1] = rs2.finish().astype(BF16)
+    backward_attention(1, 1, 1)
+    rows1 = RowSum(1)
+    rows1.start()
+    rs3 = ReduceScatter(3, normed_term(1))
+    rs3.start()
+    rows1.middle()
+    ag[M1].middle()
     rs3.middle()
-    ag[M1].middle()
-    normed_grad = rs3.finish()
-    result, gain_term1 = backward_result(1, normed_grad, rows1.finish())
-    out_backward[0, 0] = result
-    gain_all[0] = jnp.broadcast_to(gain_term0 + gain_term1, (8, BLK))
-    gain_ids = [send(gain_all.at[0], gain_all.at[n], xdev(n)) for n in range(1, REPLICAS)]
     ag[M1].finish()
     ag[M1].last()
     out_forward[0, 0] = output_projection(M1, gath[F1, c, 0])
+    normed_grad = rs3.finish()
+    result, gain_term1 = backward_result(1, normed_grad, rows1.finish())
+    gain_all[0] = jnp.broadcast_to(gain_term0 + gain_term1, (8, BLK))
+    gain_ids = [send(gain_all.at[0], gain_all.at[n], xdev(n)) for n in range(1, REPLICAS)]
+    out_backward[0, 0] = result
     total = gain_all[0]
     for n in range(1, REPLICAS):
         arrive(gain_ids[n - 1], gain_all.at[n])

time: 136 us -> 132 us (0.971)
  Pallas kernels: 132 us -> 128 us
    pallas_call x1, Pallas kernels: 132 us -> 128 us  [local(): pl.pallas_call(kernel, out_shape=(jax.ShapeDtypeStruct((1, 1) + block, BF...]
where the time goes in v3:
time: 132 us; the launch traced here: 131 us
  Pallas kernels  128 us (97%)
  local copies, waits for them, and re-layouts  2.71 us (2%)
    pallas_call x1, Pallas kernels, local(): pl.pallas_call(kernel, out_shape=(jax.ShapeDtypeStruct((1, 1) + block, BF...  128 us
    unnamed x7, local copies, waits for them, and re-layouts  2.71 us

profile of v3, /device:TPU:1, one launch (start us, length us, event | category | flops | bytes accessed | tf_op | source)
XLA Modules:
  0.0 130.9 jit_solution(16516939095563640536)
XLA Ops:
  0.6 127.5 %shard_map.157 = (bf16[1,1,128,256]{3,2,1,0:T(8,128)(2,1)}, bf16[1,1,128,256]{3,2,1,0:T(8,128)(2,1)}, f32[1,256]{1,0:T(1,128)}) custom-call(bf16[1,1,128,256]{3,2,1,0:T(8,128)(2,1)} %arrivals.1, bf16[2,1,128,256]{3,2,1,0:T(8,128)(2,1)} %fresh.1, bf16[2,1,1,128,256]{4,3,2,1,0:T(8,128)(2,1)} %stash.1, bf16[1,1,128,256]{3,2,1,0:T(8,128)(2,1)} %returning.1, ...), custom_call_target="tpu_custom_call" | custom-call | tf_op jit(solution)/shard_map/pallas_call | solution.py:688
  128.2 0.0 copy-start
  128.2 1.5 %copy.20 = bf16[1,1,128,256]{3,2,1,0:T(8,128)(2,1)} copy(bf16[1,1,128,256]{3,2,1,0:T(8,128)(2,1)} %get-tuple-element.6) | data formatting | bytes 131072
  129.7 0.0 copy-done
  129.7 0.0 copy-start.1
  129.7 0.6 copy.21
  130.3 0.0 copy-done.1
  130.3 0.6 copy.22
Async XLA Ops:
  128.2 1.5 %copy-start = (bf16[1,1,128,256]{3,2,1,0:T(8,128)(2,1)S(1)}, bf16[1,1,128,256]{3,2,1,0:T(8,128)(2,1)}, u32[]{:S(2)}) copy-start(bf16[1,1,128,256]{3,2,1,0:T(8,128)(2,1)} %get-tuple-element.7) | copy-start | bytes 196612
  129.7 0.6 copy-start.1

commit v4 on v3

--- a/solution.py
+++ b/solution.py
@@ -83,6 +83,11 @@
     row_sib,
     row_all,
     gain_all,
+    probs_buf,
+    loss,
+    term_own,
+    term_x,
+    term_z,
     ss,
     rs,
     ls,
@@ -138,14 +143,20 @@
     load_wq = pltpu.make_async_copy(query_weight.at[0], wq.at[own], ls.at[1])
     load_key = pltpu.make_async_copy(key_weight.at[0], kv.at[c, d, pl.ds(0, 64)], ls.at[2])
     load_value = pltpu.make_async_copy(value_weight.at[0], kv.at[c, d, pl.ds(64, 64)], ls.at[3])
-    for load in (load_key, load_value, load_wq, load_ow):
-        load.start()
 
     peers = [zdev(k) for k in range(1, RING)] + [sibling]
     peers += [xdev(k) for k in range(1, REPLICAS)] + [ydev(1), ydev(-1)]
     barrier = pltpu.get_barrier_semaphore()
     for peer in peers:
         pl.semaphore_signal(barrier, inc=1, device_id=peer, device_id_type=MESH)
+    load_s0 = pltpu.make_async_copy(stash.at[0, 0, 0], gath.at[S0, c, 0], ls.at[4])
+    load_s1 = pltpu.make_async_copy(stash.at[1, 0, 0], gath.at[S1, c, 0], ls.at[5])
+    load_loss = pltpu.make_async_copy(loss_grad.at[pl.ds(0, TICKS), 0], loss, ls.at[6])
+    load_fresh = pltpu.make_async_copy(
+        fresh.at[pl.ds(0, TICKS), 0], fr.at[pl.ds(0, TICKS), d], ls.at[7]
+    )
+    for load in (load_s0, load_s1, load_loss, load_fresh, load_key, load_value, load_wq, load_ow):
+        load.start()
     pl.semaphore_wait(barrier, len(peers))
 
     def replica(k):
@@ -249,8 +260,8 @@
     ag = [AllGather(gath.at[i], ROWS // 2) for i in range(6)]
     ag_gain = AllGather(gains, 8)
 
-    gath[S0, c, 0] = stash[0, 0, 0]
-    gath[S1, c, 0] = stash[1, 0, 0]
+    load_s0.wait()
+    load_s1.wait()
     gains[c, 0] = jnp.broadcast_to(gain[...], (16, BLK))
     ag_gain.start()
     ag[S0].start()
@@ -261,7 +272,6 @@
     @pl.when(s == 0)
     def _():
         for k in range(TICKS):
-            fr[k, d] = fresh[k, 0]
             for n in range(3):
                 describe(fresh.at[k, 0], fr.at[k, d], fresh_ids[k][n], xdev(n + 1)).start()
 
@@ -297,8 +307,10 @@
         new = first_docs if k == 0 else jnp.where(s == 0, balanced(1), first_docs)
         store_mask(2 + k, jnp.where(s > k, arrived, new))
 
+    load_loss.wait()
+    load_fresh.wait()
     arrive(y_backward, yrecv.at[1])
-    grad_in[0] = jnp.where(s == SECTIONS - 1, loss_grad[0, 0], yrecv[1])
+    grad_in[0] = jnp.where(s == SECTIONS - 1, loss[0], yrecv[1])
     arrive(y_forward, yrecv.at[0])
 
     @pl.when(s == 0)
@@ -340,7 +352,7 @@
 
             lax.fori_loop(low, high, body, 0, unroll=high - low)
 
-        def start(self):
+        def start(self, between=None):
             n = self.n
             away, near = pl.ds(5, 3), pl.ds(0, 5)
             self.fill(part_sib, 1 - c, 5, 8)
@@ -356,6 +368,8 @@
             self.rb = send(part.at[n, 6], relay.at[n, 1], zdev(1))
             self.ha = send(part.at[n, 7, low], relay_half.at[n, 0], zdev(-2))
             self.hb = send(part.at[n, 7, high], relay_half.at[n, 1], zdev(2))
+            if between is not None:
+                between()
             self.fill(part, c, 0, 5)
             arrive(self.k0, recv_sib.at[n, near])
             for p in (1, 2):
@@ -491,8 +505,9 @@
         mixed = dot_nn(probs.astype(BF16), proj[slot, 3]).astype(BF16)
         gath[index, c, 0] = jnp.concatenate([mixed[:ROWS], mixed[ROWS:]], axis=1)
 
-    def backward_attention(slot, mask, k):
-        q2, probs = attention(slot, mask)
+    def backward_attention(slot, k):
+        q2 = jnp.concatenate([proj[slot, 0], proj[slot, 1]], axis=0)
+        probs = probs_buf[...]
         key, value = proj[slot, 2], proj[slot, 3]
         hg = head_grad[k]
         hg2 = jnp.concatenate([hg[:, :HEAD], hg[:, HEAD:]], axis=0)
@@ -537,13 +552,12 @@
             return jnp.broadcast_to(total[:1], (ROWS, ROWS)).T
 
     def backward_result(k, normed_grad, row):
-        h = stash[k, 0, 0].astype(F32)
+        h = gath[(S0, S1)[k], c, 0].astype(F32)
         inv = inv_buf[k][:, :1]
         scaled = normed_grad * gain[...]
         factor = inv * inv * row[:, :1] * (1.0 / MODEL_WIDTH)
         result = grad_in[k].astype(F32) + inv * scaled - h * factor
-        term = jnp.sum(normed_grad * (h * inv), axis=0, keepdims=True)
-        return result.astype(BF16), term
+        return result.astype(BF16), h * inv
 
     def output_projection(index, hidden):
         acc = hidden.astype(F32)
@@ -571,7 +585,8 @@
     project.done()
     forward_attention(2, 2, M0)
     ag[M0].start()
-    backward_attention(0, 0, 0)
+    probs_buf[...] = attention(0, 0)[1]
+    backward_attention(0, 0)
     rows0 = RowSum(0)
     rows0.start()
     rs1 = ReduceScatter(1, normed_term(0))
@@ -583,10 +598,13 @@
     ag[M0].last()
     ysend[0] = output_projection(M0, gath[F0, c, 0])
     y_forward = send(ysend.at[0], yrecv.at[2], ydev(1))
+    probs_buf[...] = attention(1, 1)[1]
     normed_grad = rs1.finish()
-    result, gain_term0 = backward_result(0, normed_grad, rows0.finish())
+    result, unit = backward_result(0, normed_grad, rows0.finish())
     ysend[1] = result
     y_backward = send(ysend.at[1], yrecv.at[3], ydev(-1))
+    gain_all[0] = jnp.broadcast_to(jnp.sum(normed_grad * unit, axis=0, keepdims=True), (8, BLK))
+    gain_ids = [send(gain_all.at[0], gain_all.at[n], xdev(n)) for n in range(1, REPLICAS)]
 
     arrive(y_forward, yrecv.at[2])
 
@@ -600,7 +618,7 @@
 
     ag[F1].start()
     arrive(y_backward, yrecv.at[3])
-    grad_in[1] = jnp.where(s == SECTIONS - 1, loss_grad[1, 0], yrecv[3])
+    grad_in[1] = jnp.where(s == SECTIONS - 1, loss[1], yrecv[3])
     rs2 = ReduceScatter(2, head_term(1))
     rs2.start()
     ag[F1].middle()
@@ -614,26 +632,40 @@
     forward_attention(3, 3, M1)
     ag[M1].start()
     head_grad[1] = rs2.finish().astype(BF16)
-    backward_attention(1, 1, 1)
+    backward_attention(1, 1)
     rows1 = RowSum(1)
     rows1.start()
     rs3 = ReduceScatter(3, normed_term(1))
-    rs3.start()
+    rs3.start(ag[M1].middle)
     rows1.middle()
-    ag[M1].middle()
+    inv1 = inv_buf[1][:, :1]
+    for p in range(RING):
+        piece = part[3, p].astype(F32)
+        if p in (0, 3, 4):
+            piece = piece + recv_sib[3, p].astype(F32)
+        unit = gath[S1, c, p].astype(F32) * inv1
+        term_own[p] = jnp.broadcast_to(jnp.sum(piece * unit, axis=0, keepdims=True), (8, BLK))
+    term_ids = [send(term_own, term_x.at[n], xdev(n)) for n in range(1, REPLICAS)]
     rs3.middle()
+    for n in range(1, REPLICAS):
+        arrive(term_ids[n - 1], term_x.at[n])
+    term_x[0] = term_own[...] + term_x[1] + term_x[2] + term_x[3]
+    term_ids = []
+    for p, off, back in ((1, -1, 2), (2, 1, 1), (3, -2, 4), (4, 2, 3), (5, -3, 6), (6, 3, 5), (7, 4, 7)):
+        term_ids.append((send(term_x.at[0, p], term_z.at[back], zdev(off)), back))
     ag[M1].finish()
     ag[M1].last()
     out_forward[0, 0] = output_projection(M1, gath[F1, c, 0])
     normed_grad = rs3.finish()
-    result, gain_term1 = backward_result(1, normed_grad, rows1.finish())
-    gain_all[0] = jnp.broadcast_to(gain_term0 + gain_term1, (8, BLK))
-    gain_ids = [send(gain_all.at[0], gain_all.at[n], xdev(n)) for n in range(1, REPLICAS)]
+    result, unit = backward_result(1, normed_grad, rows1.finish())
     out_backward[0, 0] = result
-    total = gain_all[0]
+    total = gain_all[0] + term_x[0, 0]
     for n in range(1, REPLICAS):
         arrive(gain_ids[n - 1], gain_all.at[n])
         total = total + gain_all[n]
+    for i, back in term_ids:
+        arrive(i, term_z.at[back])
+        total = total + term_z[back]
     out_gain[...] = total[:1] * (1.0 / math.sqrt(TICKS * REPLICAS * ROWS))
 
     for copy in sends:
@@ -650,7 +682,7 @@
     vmem = pl.BlockSpec(memory_space=pltpu.VMEM)
     anywhere = pl.BlockSpec(memory_space=pl.ANY)
     smem = pl.BlockSpec(memory_space=pltpu.SMEM)
-    in_specs = [vmem] * 6 + [anywhere] * 4 + [smem, vmem, vmem, vmem]
+    in_specs = [anywhere] * 5 + [vmem] + [anywhere] * 4 + [smem, vmem, vmem, vmem]
     arguments = list(arguments)
     for n in (7, 8):
         arguments[n] = jnp.swapaxes(arguments[n], 1, 2)
@@ -681,9 +713,14 @@
         pltpu.VMEM((TICKS, 8, ROWS), F32),
         pltpu.VMEM((TICKS, RING, 8, ROWS), F32),
         pltpu.VMEM((REPLICAS, 8, BLK), F32),
+        pltpu.VMEM((2 * ROWS, ROWS), F32),
+        pltpu.VMEM((TICKS,) + block, BF16),
+        pltpu.VMEM((RING, 8, BLK), F32),
+        pltpu.VMEM((REPLICAS, RING, 8, BLK), F32),
+        pltpu.VMEM((RING, 8, BLK), F32),
         pltpu.SemaphoreType.DMA((SEMS,)),
         pltpu.SemaphoreType.DMA((SEMS,)),
-        pltpu.SemaphoreType.DMA((4,)),
+        pltpu.SemaphoreType.DMA((8,)),
     ]
     return pl.pallas_call(
         kernel,

time: 132 us -> 131 us (level)
  Pallas kernels: 128 us -> 126 us
where the time goes in v4:
time: 131 us; the launch traced here: 130 us
  Pallas kernels  126 us (96%)
  local copies, waits for them, and re-layouts  2.71 us (2%)
    pallas_call x1, Pallas kernels, local(): pl.pallas_call(kernel, out_shape=(jax.ShapeDtypeStruct((1, 1) + block, BF...  126 us
    unnamed x7, local copies, waits for them, and re-layouts  2.71 us

profile of v4, /device:TPU:1, one launch (start us, length us, event | category | flops | bytes accessed | tf_op | source)
XLA Modules:
  0.0 129.8 jit_solution(13255045999393045277)
XLA Ops:
  0.6 126.4 %shard_map.157 = (bf16[1,1,128,256]{3,2,1,0:T(8,128)(2,1)}, bf16[1,1,128,256]{3,2,1,0:T(8,128)(2,1)}, f32[1,256]{1,0:T(1,128)}) custom-call(bf16[1,1,128,256]{3,2,1,0:T(8,128)(2,1)} %arrivals.1, bf16[2,1,128,256]{3,2,1,0:T(8,128)(2,1)} %fresh.1, bf16[2,1,1,128,256]{4,3,2,1,0:T(8,128)(2,1)} %stash.1, bf16[1,1,128,256]{3,2,1,0:T(8,128)(2,1)} %returning.1, ...), custom_call_target="tpu_custom_call" | custom-call | tf_op jit(solution)/shard_map/pallas_call | solution.py:725
  127.1 0.0 copy-start
  127.1 1.5 %copy.20 = bf16[1,1,128,256]{3,2,1,0:T(8,128)(2,1)} copy(bf16[1,1,128,256]{3,2,1,0:T(8,128)(2,1)} %get-tuple-element.6) | data formatting | bytes 131072
  128.6 0.0 copy-done
  128.6 0.0 copy-start.1
  128.6 0.6 copy.21
  129.2 0.0 copy-done.1
  129.2 0.6 copy.22
Async XLA Ops:
  127.1 1.5 %copy-start = (bf16[1,1,128,256]{3,2,1,0:T(8,128)(2,1)S(1)}, bf16[1,1,128,256]{3,2,1,0:T(8,128)(2,1)}, u32[]{:S(2)}) copy-start(bf16[1,1,128,256]{3,2,1,0:T(8,128)(2,1)} %get-tuple-element.7) | copy-start | bytes 196612
  128.6 0.6 copy-start.1

commit v5 on v4

--- a/solution.py
+++ b/solution.py
@@ -598,7 +598,6 @@
     ag[M0].last()
     ysend[0] = output_projection(M0, gath[F0, c, 0])
     y_forward = send(ysend.at[0], yrecv.at[2], ydev(1))
-    probs_buf[...] = attention(1, 1)[1]
     normed_grad = rs1.finish()
     result, unit = backward_result(0, normed_grad, rows0.finish())
     ysend[1] = result
@@ -617,11 +616,11 @@
         gath[F1, c, 0] = yrecv[2]
 
     ag[F1].start()
+    probs_buf[...] = attention(1, 1)[1]
     arrive(y_backward, yrecv.at[3])
     grad_in[1] = jnp.where(s == SECTIONS - 1, loss[1], yrecv[3])
     rs2 = ReduceScatter(2, head_term(1))
-    rs2.start()
-    ag[F1].middle()
+    rs2.start(ag[F1].middle)
     rs2.middle()
     ag[F1].finish()
     ag[F1].last()

time: 131 us -> 128 us (0.977)
  Pallas kernels: 126 us -> 124 us
    pallas_call x1, Pallas kernels: 126 us -> 124 us  [local(): pl.pallas_call(kernel, out_shape=(jax.ShapeDtypeStruct((1, 1) + block, BF...]
where the time goes in v5:
time: 128 us
  Pallas kernels  124 us (97%)
  local copies, waits for them, and re-layouts  2.71 us (2%)
    pallas_call x1, Pallas kernels, local(): pl.pallas_call(kernel, out_shape=(jax.ShapeDtypeStruct((1, 1) + block, BF...  124 us
    unnamed x7, local copies, waits for them, and re-layouts  2.71 us

profile of v5, /device:TPU:1, one launch (start us, length us, event | category | flops | bytes accessed | tf_op | source)
XLA Modules:
  0.0 127.6 jit_solution(4616541594852912081)
XLA Ops:
  0.6 124.2 %shard_map.157 = (bf16[1,1,128,256]{3,2,1,0:T(8,128)(2,1)}, bf16[1,1,128,256]{3,2,1,0:T(8,128)(2,1)}, f32[1,256]{1,0:T(1,128)}) custom-call(bf16[1,1,128,256]{3,2,1,0:T(8,128)(2,1)} %arrivals.1, bf16[2,1,128,256]{3,2,1,0:T(8,128)(2,1)} %fresh.1, bf16[2,1,1,128,256]{4,3,2,1,0:T(8,128)(2,1)} %stash.1, bf16[1,1,128,256]{3,2,1,0:T(8,128)(2,1)} %returning.1, ...), custom_call_target="tpu_custom_call" | custom-call | tf_op jit(solution)/shard_map/pallas_call | solution.py:724
  124.8 0.0 copy-start
  124.9 1.5 %copy.20 = bf16[1,1,128,256]{3,2,1,0:T(8,128)(2,1)} copy(bf16[1,1,128,256]{3,2,1,0:T(8,128)(2,1)} %get-tuple-element.6) | data formatting | bytes 131072
  126.4 0.0 copy-done
  126.4 0.0 copy-start.1
  126.4 0.6 copy.21
  127.0 0.0 copy-done.1
  127.0 0.6 copy.22
Async XLA Ops:
  124.8 1.5 %copy-start = (bf16[1,1,128,256]{3,2,1,0:T(8,128)(2,1)S(1)}, bf16[1,1,128,256]{3,2,1,0:T(8,128)(2,1)}, u32[]{:S(2)}) copy-start(bf16[1,1,128,256]{3,2,1,0:T(8,128)(2,1)} %get-tuple-element.7) | copy-start | bytes 196612
  126.4 0.6 copy-start.1
